TPU v7x, 512 devices: a whole 4x8x8 slice. The times are simulated.
512 devices in a mesh: space: 64 (over z, x, y_lo), sta: 8 (over y_hi, core).
Axes of the slice: x: 4, y: 8 (y_hi: 4, y_lo: 2; y = y_hi * 2 + y_lo), z: 8, core: 2. Of those that a mesh axis runs over, the one named last changes fastest.
Arguments:
- coarse_times: float32 [16, 320, 32, 128], P('sta', 'space'), as said below
- model_map: int32 [320, 32, 128], P('space'), may hold values from 0 to 63
- slowness: float32 [64], replicated, may hold values from 0.12 to 0.3
- picks: float32 [256, 16], replicated
- pick_mask: int32 [256, 16], replicated, may hold values from 0 to 1, as said below
Outputs:
- refined: float32 [16, 320, 32, 128], P(None, 'space', 'sta')
- density: float32 [256, 320, 32, 128], P(None, 'space', 'sta')
Inputs may be any that keep to these rules, and one draw needn't show every extreme that they name: `pick_mask`: each event has at least 4 stations with a pick. `coarse_times`: zero at each station's own cell and positive elsewhere.
All inputs are finite; a program needn't handle non-finite values.
Results may differ from a plain program's by a relative error of at most 0.0003.
Values sent between devices are 32-bit elements; how exact they have to be, the bound alone decides.
A program may use at most 64 MiB of HBM per device.

v0:
```python
import jax
import jax.numpy as jnp
from jax import lax
from jax.sharding import PartitionSpec as P

ROUNDS = 12


BIG = 1000000.0
pick_sigma = 0.25
grid_step = 1.0
block_events = 32


def extended_2(block, sides, width):
    for axis, dim in sides:
        count = lax.axis_size(axis)
        forward = [(i, i + 1) for i in range(count - 1)]
        backward = [(target, source) for source, target in forward]
        low = lax.ppermute(
            lax.slice_in_dim(block, block.shape[dim] - width, None, axis=dim), axis, forward
        )
        high = lax.ppermute(lax.slice_in_dim(block, 0, width, axis=dim), axis, backward)
        block = jnp.concatenate([low, block, high], axis=dim)
    return block


def godunov(near_one, near_two, near_three, speed):
    lowest = jnp.minimum(jnp.minimum(near_one, near_two), near_three)
    highest = jnp.maximum(jnp.maximum(near_one, near_two), near_three)
    middle = jnp.maximum(
        jnp.minimum(near_one, near_two), jnp.minimum(jnp.maximum(near_one, near_two), near_three)
    )
    gap_mid = middle - lowest
    gap_high = highest - lowest
    two_sided = 0.5 * (
        gap_mid + jnp.sqrt(jnp.maximum(2.0 * speed * speed - gap_mid * gap_mid, 0.0))
    )
    gap_sum = gap_mid + gap_high
    squares = gap_mid * gap_mid + gap_high * gap_high - speed * speed
    three_sided = (gap_sum + jnp.sqrt(jnp.maximum(gap_sum * gap_sum - 3.0 * squares, 0.0))) / 3.0
    increase = jnp.where(
        speed <= gap_mid, speed, jnp.where(two_sided <= gap_high, two_sided, three_sided)
    )
    return lowest + increase


def relax(extended, speed):
    centre = extended[:, 1:-1]
    along_x = jnp.minimum(extended[:, :-2], extended[:, 2:])
    padded = jnp.pad(centre, ((0, 0), (0, 0), (1, 1), (1, 1)), constant_values=BIG)
    along_y = jnp.minimum(padded[:, :, :-2, 1:-1], padded[:, :, 2:, 1:-1])
    along_z = jnp.minimum(padded[:, :, 1:-1, :-2], padded[:, :, 1:-1, 2:])
    return jnp.minimum(centre, godunov(along_x, along_y, along_z, speed[None]))


def close_rims(extended, rim_width, at_lower, at_upper):
    cell_count = extended.shape[1]
    position = lax.broadcasted_iota(jnp.int32, (1, cell_count, 1, 1), 1)
    outside = (position < rim_width) & at_lower | (position >= cell_count - rim_width) & at_upper
    return jnp.where(outside, BIG, extended)


def misfit_block(event_pair, flat_tables):
    arrivals, observed = event_pair
    pick_count = jnp.sum(observed, 1)
    residual = arrivals[:, :, None] - flat_tables[None]
    anchor_shift = jnp.sum(observed[:, :, None] * residual, 1) / pick_count[:, None]
    deviation = residual - anchor_shift[:, None, :]
    return jnp.sum(observed[:, :, None] * deviation * deviation, 1)


def body(coarse_times, model_map, slowness, picks, pick_mask):
    levels = lax.broadcasted_iota(jnp.int32, (slowness.shape[0], 1, 1, 1), 0)
    speed = grid_step * jnp.sum(
        jnp.where(model_map[None] == levels, slowness[:, None, None, None], 0.0), 0
    )
    position_space = lax.axis_index("space")
    devices_space = lax.axis_size("space")
    at_lower = position_space == 0
    at_upper = position_space == devices_space - 1
    tables = coarse_times

    def one_round(round_index, tables):
        extended = extended_2(tables, (("space", 1),), 1)
        return relax(close_rims(extended, 1, at_lower, at_upper), speed)

    tables = lax.fori_loop(0, ROUNDS, one_round, tables)
    refined = lax.all_to_all(tables, "sta", split_axis=2, concat_axis=0, tiled=True)
    stations = refined.shape[0]
    flat_tables = refined.reshape(stations, -1)
    observed = pick_mask.astype(jnp.float32)
    blocks = lax.map(
        lambda event_pair: misfit_block(event_pair, flat_tables),
        (picks.reshape(-1, block_events, stations), observed.reshape(-1, block_events, stations)),
    )
    score = -0.5 * blocks.reshape(picks.shape[0], -1) / (pick_sigma * pick_sigma)
    local_top = jnp.max(score, 1)
    top_score = lax.pmax(local_top, ("space", "sta"))
    cell_weights = jnp.exp(score - top_score[:, None])
    mass_sum = lax.psum(jnp.sum(cell_weights, 1), ("space", "sta"))
    density = cell_weights / mass_sum[:, None]
    density = density.reshape(picks.shape[0], refined.shape[1], refined.shape[2], refined.shape[3])
    return (refined, density)


def solution(mesh):
    placed = (P("sta", "space", None, None), P("space", None, None), P(), P(), P())
    return jax.shard_map(
        body,
        mesh=mesh,
        in_specs=placed,
        out_specs=(P(None, "space", "sta", None), P(None, "space", "sta", None)),
        check_vma=False,
    )
```

profile of v0, /device:TPU:1, one launch (start us, length us, event | category | flops | bytes accessed | tf_op | source)
XLA Modules:
  0.0 400.3 jit_solution(15108687910519187585)
XLA Ops:
  1.5 1.5 select_reduce_fusion
  3.1 96.4 %while.22 = (s32[]{:T(128)}, f32[2,5,32,128]{3,2,1,0:T(8,128)S(1)}, pred[]{:T(512)}, pred[]{:T(512)}, f32[5,32,128]{2,1,0:T(8,128)S(1)}, /*index=5*/f32[1,5,32,128]{3,2,1,0:T(8,128)S(1)}, s32[]{:T(128)}) while((s32[]{:T(128)}, f32[2,5,32,128]{3,2,1,0:T(8,128)S(1)}, pred[]{:T(512)}, pred[]{:T(512)}, f32[5,32,128]{2,1,0:T(8,128)S(1)}, ...), condition=%wide.region_2.3_spmd, body=%wide.region_1.2_spmd.sunk | while | flops 1523749 | bytes 2244781 | solution.py:88
  3.1 1.3 collective-permute-start
  4.4 4.6 %collective-permute-start.1 = (f32[2,1,32,128]{3,2,1,0:T(8,128)S(1)}, f32[2,1,32,128]{3,2,1,0:T(8,128)S(1)}, u32[]{:S(2)}, u32[]{:S(2)}) collective-permute-start(f32[2,1,32,128]{3,2,1,0:T(8,128)S(1)} %get-tuple-element.226), channel_id=1, source_target_pairs={{0,8},{8,16},{16,24},{24,32},{32,40},{40,48},{48,56},{56,64},{64,7... | collective-permute-start | bytes 98312 | tf_op jit(solution)/shard_map/while/body/eval_jaxpr/ppermute | solution.py:20
  10.6 1.3 collective-permute-start
  11.9 4.9 %collective-permute-start.1 = (f32[2,1,32,128]{3,2,1,0:T(8,128)S(1)}, f32[2,1,32,128]{3,2,1,0:T(8,128)S(1)}, u32[]{:S(2)}, u32[]{:S(2)}) collective-permute-start(f32[2,1,32,128]{3,2,1,0:T(8,128)S(1)} %get-tuple-element.226), channel_id=1, source_target_pairs={{0,8},{8,16},{16,24},{24,32},{32,40},{40,48},{48,56},{56,64},{64,7... | collective-permute-start | bytes 98312 | tf_op jit(solution)/shard_map/while/body/eval_jaxpr/ppermute | solution.py:20
  19.5 5.2 %collective-permute-start.1 = (f32[2,1,32,128]{3,2,1,0:T(8,128)S(1)}, f32[2,1,32,128]{3,2,1,0:T(8,128)S(1)}, u32[]{:S(2)}, u32[]{:S(2)}) collective-permute-start(f32[2,1,32,128]{3,2,1,0:T(8,128)S(1)} %get-tuple-element.226), channel_id=1, source_target_pairs={{0,8},{8,16},{16,24},{24,32},{32,40},{40,48},{48,56},{56,64},{64,7... | collective-permute-start | bytes 98312 | tf_op jit(solution)/shard_map/while/body/eval_jaxpr/ppermute | solution.py:20
  27.5 5.2 %collective-permute-start.1 = (f32[2,1,32,128]{3,2,1,0:T(8,128)S(1)}, f32[2,1,32,128]{3,2,1,0:T(8,128)S(1)}, u32[]{:S(2)}, u32[]{:S(2)}) collective-permute-start(f32[2,1,32,128]{3,2,1,0:T(8,128)S(1)} %get-tuple-element.226), channel_id=1, source_target_pairs={{0,8},{8,16},{16,24},{24,32},{32,40},{40,48},{48,56},{56,64},{64,7... | collective-permute-start | bytes 98312 | tf_op jit(solution)/shard_map/while/body/eval_jaxpr/ppermute | solution.py:20
  35.5 5.2 %collective-permute-start.1 = (f32[2,1,32,128]{3,2,1,0:T(8,128)S(1)}, f32[2,1,32,128]{3,2,1,0:T(8,128)S(1)}, u32[]{:S(2)}, u32[]{:S(2)}) collective-permute-start(f32[2,1,32,128]{3,2,1,0:T(8,128)S(1)} %get-tuple-element.226), channel_id=1, source_target_pairs={{0,8},{8,16},{16,24},{24,32},{32,40},{40,48},{48,56},{56,64},{64,7... | collective-permute-start | bytes 98312 | tf_op jit(solution)/shard_map/while/body/eval_jaxpr/ppermute | solution.py:20
  43.4 5.2 %collective-permute-start.1 = (f32[2,1,32,128]{3,2,1,0:T(8,128)S(1)}, f32[2,1,32,128]{3,2,1,0:T(8,128)S(1)}, u32[]{:S(2)}, u32[]{:S(2)}) collective-permute-start(f32[2,1,32,128]{3,2,1,0:T(8,128)S(1)} %get-tuple-element.226), channel_id=1, source_target_pairs={{0,8},{8,16},{16,24},{24,32},{32,40},{40,48},{48,56},{56,64},{64,7... | collective-permute-start | bytes 98312 | tf_op jit(solution)/shard_map/while/body/eval_jaxpr/ppermute | solution.py:20
  51.4 5.2 %collective-permute-start.1 = (f32[2,1,32,128]{3,2,1,0:T(8,128)S(1)}, f32[2,1,32,128]{3,2,1,0:T(8,128)S(1)}, u32[]{:S(2)}, u32[]{:S(2)}) collective-permute-start(f32[2,1,32,128]{3,2,1,0:T(8,128)S(1)} %get-tuple-element.226), channel_id=1, source_target_pairs={{0,8},{8,16},{16,24},{24,32},{32,40},{40,48},{48,56},{56,64},{64,7... | collective-permute-start | bytes 98312 | tf_op jit(solution)/shard_map/while/body/eval_jaxpr/ppermute | solution.py:20
  59.4 5.2 %collective-permute-start.1 = (f32[2,1,32,128]{3,2,1,0:T(8,128)S(1)}, f32[2,1,32,128]{3,2,1,0:T(8,128)S(1)}, u32[]{:S(2)}, u32[]{:S(2)}) collective-permute-start(f32[2,1,32,128]{3,2,1,0:T(8,128)S(1)} %get-tuple-element.226), channel_id=1, source_target_pairs={{0,8},{8,16},{16,24},{24,32},{32,40},{40,48},{48,56},{56,64},{64,7... | collective-permute-start | bytes 98312 | tf_op jit(solution)/shard_map/while/body/eval_jaxpr/ppermute | solution.py:20
  67.3 5.3 %collective-permute-start.1 = (f32[2,1,32,128]{3,2,1,0:T(8,128)S(1)}, f32[2,1,32,128]{3,2,1,0:T(8,128)S(1)}, u32[]{:S(2)}, u32[]{:S(2)}) collective-permute-start(f32[2,1,32,128]{3,2,1,0:T(8,128)S(1)} %get-tuple-element.226), channel_id=1, source_target_pairs={{0,8},{8,16},{16,24},{24,32},{32,40},{40,48},{48,56},{56,64},{64,7... | collective-permute-start | bytes 98312 | tf_op jit(solution)/shard_map/while/body/eval_jaxpr/ppermute | solution.py:20
  75.4 5.3 %collective-permute-start.1 = (f32[2,1,32,128]{3,2,1,0:T(8,128)S(1)}, f32[2,1,32,128]{3,2,1,0:T(8,128)S(1)}, u32[]{:S(2)}, u32[]{:S(2)}) collective-permute-start(f32[2,1,32,128]{3,2,1,0:T(8,128)S(1)} %get-tuple-element.226), channel_id=1, source_target_pairs={{0,8},{8,16},{16,24},{24,32},{32,40},{40,48},{48,56},{56,64},{64,7... | collective-permute-start | bytes 98312 | tf_op jit(solution)/shard_map/while/body/eval_jaxpr/ppermute | solution.py:20
  83.5 5.2 %collective-permute-start.1 = (f32[2,1,32,128]{3,2,1,0:T(8,128)S(1)}, f32[2,1,32,128]{3,2,1,0:T(8,128)S(1)}, u32[]{:S(2)}, u32[]{:S(2)}) collective-permute-start(f32[2,1,32,128]{3,2,1,0:T(8,128)S(1)} %get-tuple-element.226), channel_id=1, source_target_pairs={{0,8},{8,16},{16,24},{24,32},{32,40},{40,48},{48,56},{56,64},{64,7... | collective-permute-start | bytes 98312 | tf_op jit(solution)/shard_map/while/body/eval_jaxpr/ppermute | solution.py:20
  91.5 6.5 %collective-permute-start.1 = (f32[2,1,32,128]{3,2,1,0:T(8,128)S(1)}, f32[2,1,32,128]{3,2,1,0:T(8,128)S(1)}, u32[]{:S(2)}, u32[]{:S(2)}) collective-permute-start(f32[2,1,32,128]{3,2,1,0:T(8,128)S(1)} %get-tuple-element.226), channel_id=1, source_target_pairs={{0,8},{8,16},{16,24},{24,32},{32,40},{40,48},{48,56},{56,64},{64,7... | collective-permute-start | bytes 98312 | tf_op jit(solution)/shard_map/while/body/eval_jaxpr/ppermute | solution.py:20
  100.3 20.7 %all-to-all-start = ((f32[2,5,32,128]{3,0,1,2:T(2,128)}), f32[2,5,32,128]{3,0,1,2:T(2,128)S(1)}, u32[]{:S(2)}, u32[]{:S(2)}) async-start(f32[2,5,32,128]{3,0,1,2:T(2,128)} %copy.27), calls=%async_computation | async-start | bytes 327680 | tf_op jit(solution)/shard_map/all_to_all | solution.py:89
  121.2 8.6 %all-to-all-done = f32[2,5,32,128]{3,0,1,2:T(2,128)S(1)} async-done(((f32[2,5,32,128]{3,0,1,2:T(2,128)}), f32[2,5,32,128]{3,0,1,2:T(2,128)S(1)}, u32[]{:S(2)}, u32[]{:S(2)}) %all-to-all-start) | async-done | bytes 163872 | tf_op jit(solution)/shard_map/all_to_all | solution.py:89
  130.4 26.5 %while.23 = (s32[]{:T(128)}, f32[8,32,2560]{2,1,0:T(8,128)S(1)}, f32[8,32,16]{1,0,2:T(8,128)S(1)}, f32[8,32,16]{1,0,2:T(8,128)S(1)}, f32[16,5,4,128]{3,2,1,0:T(4...) while((s32[]{:T(128)}, f32[8,32,2560]{2,1,0:T(8,128)S(1)}, f32[8,32,16]{1,0,2:T(8,128)S(1)}, ...), condition=%wide.wide.region_7.8_spmd, body=%wide.wide.region_3.7_spmd.sunk | while | flops 10404322 | bytes 2648417 | solution.py:93
  131.9 1.8 fusion.18
  135.3 1.8 fusion.18
  138.6 1.8 fusion.18
  141.9 1.8 fusion.18
  145.2 1.8 fusion.18
  148.5 1.8 fusion.18
  151.8 1.8 fusion.18
  155.1 1.8 fusion.18
  157.3 141.2 %pmax.7 = f32[256]{0:T(256)S(1)} all-reduce(f32[256]{0:T(256)S(1)} %reduce_max.12), channel_id=1, replica_groups=mesh['space'=64,'sta'=8] {'space','sta'}, use_global_device_ids=true, to_apply=%region_9.10 | all-reduce | flops 256 | bytes 2048 | tf_op jit(solution)/shard_map/pmax | solution.py:99
  298.5 2.0 exponential_reduce_fusion
  300.5 2.8 div.34
  303.4 94.4 %psum.7 = f32[256]{0:T(256)S(1)} all-reduce(f32[256]{0:T(256)S(1)} %reduce_sum.49), channel_id=1, replica_groups=mesh['space'=64,'sta'=8] {'space','sta'}, use_global_device_ids=true, to_apply=%region_11.12 | all-reduce | flops 256 | bytes 2048 | tf_op jit(solution)/shard_map/psum | solution.py:101
  397.8 2.5 exponential_divide_fusion
  (181 shorter events, 45.1 us)
Async XLA Ops:
  3.1 117.9 %copy-start.2 = (s32[256,16]{0,1:T(8,128)S(1)}, s32[256,16]{0,1:T(8,128)}, u32[]{:S(2)}) copy-start(s32[256,16]{0,1:T(8,128)} %param.13) | copy-start | bytes 49156
  3.1 118.0 %copy-start.1 = (f32[256,16]{0,1:T(8,128)S(1)}, f32[256,16]{0,1:T(8,128)}, u32[]{:S(2)}) copy-start(f32[256,16]{0,1:T(8,128)} %param.12) | copy-start | bytes 49156
  3.1 6.0 %collective-permute-start = (f32[2,1,32,128]{3,2,1,0:T(8,128)S(1)}, f32[2,1,32,128]{3,2,1,0:T(8,128)S(1)}, u32[]{:S(2)}, u32[]{:S(2)}) collective-permute-start(f32[2,1,32,128]{3,2,1,0:T(8,128)S(1)} %get-tuple-element.225), channel_id=1, source_target_pairs={{8,0},{16,8},{24,16},{32,24},{40,32},{48,40},{56,48},{64,56},{72,6... | collective-permute-start | bytes 98312 | tf_op jit(solution)/shard_map/while/body/eval_jaxpr/ppermute | solution.py:23
  4.4 5.7 %collective-permute-start.1 = (f32[2,1,32,128]{3,2,1,0:T(8,128)S(1)}, f32[2,1,32,128]{3,2,1,0:T(8,128)S(1)}, u32[]{:S(2)}, u32[]{:S(2)}) collective-permute-start(f32[2,1,32,128]{3,2,1,0:T(8,128)S(1)} %get-tuple-element.226), channel_id=1, source_target_pairs={{0,8},{8,16},{16,24},{24,32},{32,40},{40,48},{48,56},{56,64},{64,7... | collective-permute-start | bytes 98312 | tf_op jit(solution)/shard_map/while/body/eval_jaxpr/ppermute | solution.py:20
  10.6 6.2 %collective-permute-start = (f32[2,1,32,128]{3,2,1,0:T(8,128)S(1)}, f32[2,1,32,128]{3,2,1,0:T(8,128)S(1)}, u32[]{:S(2)}, u32[]{:S(2)}) collective-permute-start(f32[2,1,32,128]{3,2,1,0:T(8,128)S(1)} %get-tuple-element.225), channel_id=1, source_target_pairs={{8,0},{16,8},{24,16},{32,24},{40,32},{48,40},{56,48},{64,56},{72,6... | collective-permute-start | bytes 98312 | tf_op jit(solution)/shard_map/while/body/eval_jaxpr/ppermute | solution.py:23
  11.9 5.9 %collective-permute-start.1 = (f32[2,1,32,128]{3,2,1,0:T(8,128)S(1)}, f32[2,1,32,128]{3,2,1,0:T(8,128)S(1)}, u32[]{:S(2)}, u32[]{:S(2)}) collective-permute-start(f32[2,1,32,128]{3,2,1,0:T(8,128)S(1)} %get-tuple-element.226), channel_id=1, source_target_pairs={{0,8},{8,16},{16,24},{24,32},{32,40},{40,48},{48,56},{56,64},{64,7... | collective-permute-start | bytes 98312 | tf_op jit(solution)/shard_map/while/body/eval_jaxpr/ppermute | solution.py:20
  18.2 6.5 %collective-permute-start = (f32[2,1,32,128]{3,2,1,0:T(8,128)S(1)}, f32[2,1,32,128]{3,2,1,0:T(8,128)S(1)}, u32[]{:S(2)}, u32[]{:S(2)}) collective-permute-start(f32[2,1,32,128]{3,2,1,0:T(8,128)S(1)} %get-tuple-element.225), channel_id=1, source_target_pairs={{8,0},{16,8},{24,16},{32,24},{40,32},{48,40},{56,48},{64,56},{72,6... | collective-permute-start | bytes 98312 | tf_op jit(solution)/shard_map/while/body/eval_jaxpr/ppermute | solution.py:23
  19.5 6.2 %collective-permute-start.1 = (f32[2,1,32,128]{3,2,1,0:T(8,128)S(1)}, f32[2,1,32,128]{3,2,1,0:T(8,128)S(1)}, u32[]{:S(2)}, u32[]{:S(2)}) collective-permute-start(f32[2,1,32,128]{3,2,1,0:T(8,128)S(1)} %get-tuple-element.226), channel_id=1, source_target_pairs={{0,8},{8,16},{16,24},{24,32},{32,40},{40,48},{48,56},{56,64},{64,7... | collective-permute-start | bytes 98312 | tf_op jit(solution)/shard_map/while/body/eval_jaxpr/ppermute | solution.py:20
  26.2 6.5 %collective-permute-start = (f32[2,1,32,128]{3,2,1,0:T(8,128)S(1)}, f32[2,1,32,128]{3,2,1,0:T(8,128)S(1)}, u32[]{:S(2)}, u32[]{:S(2)}) collective-permute-start(f32[2,1,32,128]{3,2,1,0:T(8,128)S(1)} %get-tuple-element.225), channel_id=1, source_target_pairs={{8,0},{16,8},{24,16},{32,24},{40,32},{48,40},{56,48},{64,56},{72,6... | collective-permute-start | bytes 98312 | tf_op jit(solution)/shard_map/while/body/eval_jaxpr/ppermute | solution.py:23
  27.5 6.2 %collective-permute-start.1 = (f32[2,1,32,128]{3,2,1,0:T(8,128)S(1)}, f32[2,1,32,128]{3,2,1,0:T(8,128)S(1)}, u32[]{:S(2)}, u32[]{:S(2)}) collective-permute-start(f32[2,1,32,128]{3,2,1,0:T(8,128)S(1)} %get-tuple-element.226), channel_id=1, source_target_pairs={{0,8},{8,16},{16,24},{24,32},{32,40},{40,48},{48,56},{56,64},{64,7... | collective-permute-start | bytes 98312 | tf_op jit(solution)/shard_map/while/body/eval_jaxpr/ppermute | solution.py:20
  34.2 6.5 %collective-permute-start = (f32[2,1,32,128]{3,2,1,0:T(8,128)S(1)}, f32[2,1,32,128]{3,2,1,0:T(8,128)S(1)}, u32[]{:S(2)}, u32[]{:S(2)}) collective-permute-start(f32[2,1,32,128]{3,2,1,0:T(8,128)S(1)} %get-tuple-element.225), channel_id=1, source_target_pairs={{8,0},{16,8},{24,16},{32,24},{40,32},{48,40},{56,48},{64,56},{72,6... | collective-permute-start | bytes 98312 | tf_op jit(solution)/shard_map/while/body/eval_jaxpr/ppermute | solution.py:23
  35.5 6.2 %collective-permute-start.1 = (f32[2,1,32,128]{3,2,1,0:T(8,128)S(1)}, f32[2,1,32,128]{3,2,1,0:T(8,128)S(1)}, u32[]{:S(2)}, u32[]{:S(2)}) collective-permute-start(f32[2,1,32,128]{3,2,1,0:T(8,128)S(1)} %get-tuple-element.226), channel_id=1, source_target_pairs={{0,8},{8,16},{16,24},{24,32},{32,40},{40,48},{48,56},{56,64},{64,7... | collective-permute-start | bytes 98312 | tf_op jit(solution)/shard_map/while/body/eval_jaxpr/ppermute | solution.py:20
  42.1 6.5 %collective-permute-start = (f32[2,1,32,128]{3,2,1,0:T(8,128)S(1)}, f32[2,1,32,128]{3,2,1,0:T(8,128)S(1)}, u32[]{:S(2)}, u32[]{:S(2)}) collective-permute-start(f32[2,1,32,128]{3,2,1,0:T(8,128)S(1)} %get-tuple-element.225), channel_id=1, source_target_pairs={{8,0},{16,8},{24,16},{32,24},{40,32},{48,40},{56,48},{64,56},{72,6... | collective-permute-start | bytes 98312 | tf_op jit(solution)/shard_map/while/body/eval_jaxpr/ppermute | solution.py:23
  43.4 6.2 %collective-permute-start.1 = (f32[2,1,32,128]{3,2,1,0:T(8,128)S(1)}, f32[2,1,32,128]{3,2,1,0:T(8,128)S(1)}, u32[]{:S(2)}, u32[]{:S(2)}) collective-permute-start(f32[2,1,32,128]{3,2,1,0:T(8,128)S(1)} %get-tuple-element.226), channel_id=1, source_target_pairs={{0,8},{8,16},{16,24},{24,32},{32,40},{40,48},{48,56},{56,64},{64,7... | collective-permute-start | bytes 98312 | tf_op jit(solution)/shard_map/while/body/eval_jaxpr/ppermute | solution.py:20
  50.1 6.5 %collective-permute-start = (f32[2,1,32,128]{3,2,1,0:T(8,128)S(1)}, f32[2,1,32,128]{3,2,1,0:T(8,128)S(1)}, u32[]{:S(2)}, u32[]{:S(2)}) collective-permute-start(f32[2,1,32,128]{3,2,1,0:T(8,128)S(1)} %get-tuple-element.225), channel_id=1, source_target_pairs={{8,0},{16,8},{24,16},{32,24},{40,32},{48,40},{56,48},{64,56},{72,6... | collective-permute-start | bytes 98312 | tf_op jit(solution)/shard_map/while/body/eval_jaxpr/ppermute | solution.py:23
  51.4 6.2 %collective-permute-start.1 = (f32[2,1,32,128]{3,2,1,0:T(8,128)S(1)}, f32[2,1,32,128]{3,2,1,0:T(8,128)S(1)}, u32[]{:S(2)}, u32[]{:S(2)}) collective-permute-start(f32[2,1,32,128]{3,2,1,0:T(8,128)S(1)} %get-tuple-element.226), channel_id=1, source_target_pairs={{0,8},{8,16},{16,24},{24,32},{32,40},{40,48},{48,56},{56,64},{64,7... | collective-permute-start | bytes 98312 | tf_op jit(solution)/shard_map/while/body/eval_jaxpr/ppermute | solution.py:20
  58.1 6.5 %collective-permute-start = (f32[2,1,32,128]{3,2,1,0:T(8,128)S(1)}, f32[2,1,32,128]{3,2,1,0:T(8,128)S(1)}, u32[]{:S(2)}, u32[]{:S(2)}) collective-permute-start(f32[2,1,32,128]{3,2,1,0:T(8,128)S(1)} %get-tuple-element.225), channel_id=1, source_target_pairs={{8,0},{16,8},{24,16},{32,24},{40,32},{48,40},{56,48},{64,56},{72,6... | collective-permute-start | bytes 98312 | tf_op jit(solution)/shard_map/while/body/eval_jaxpr/ppermute | solution.py:23
  59.4 6.2 %collective-permute-start.1 = (f32[2,1,32,128]{3,2,1,0:T(8,128)S(1)}, f32[2,1,32,128]{3,2,1,0:T(8,128)S(1)}, u32[]{:S(2)}, u32[]{:S(2)}) collective-permute-start(f32[2,1,32,128]{3,2,1,0:T(8,128)S(1)} %get-tuple-element.226), channel_id=1, source_target_pairs={{0,8},{8,16},{16,24},{24,32},{32,40},{40,48},{48,56},{56,64},{64,7... | collective-permute-start | bytes 98312 | tf_op jit(solution)/shard_map/while/body/eval_jaxpr/ppermute | solution.py:20
  66.0 6.6 %collective-permute-start = (f32[2,1,32,128]{3,2,1,0:T(8,128)S(1)}, f32[2,1,32,128]{3,2,1,0:T(8,128)S(1)}, u32[]{:S(2)}, u32[]{:S(2)}) collective-permute-start(f32[2,1,32,128]{3,2,1,0:T(8,128)S(1)} %get-tuple-element.225), channel_id=1, source_target_pairs={{8,0},{16,8},{24,16},{32,24},{40,32},{48,40},{56,48},{64,56},{72,6... | collective-permute-start | bytes 98312 | tf_op jit(solution)/shard_map/while/body/eval_jaxpr/ppermute | solution.py:23
  67.3 6.3 %collective-permute-start.1 = (f32[2,1,32,128]{3,2,1,0:T(8,128)S(1)}, f32[2,1,32,128]{3,2,1,0:T(8,128)S(1)}, u32[]{:S(2)}, u32[]{:S(2)}) collective-permute-start(f32[2,1,32,128]{3,2,1,0:T(8,128)S(1)} %get-tuple-element.226), channel_id=1, source_target_pairs={{0,8},{8,16},{16,24},{24,32},{32,40},{40,48},{48,56},{56,64},{64,7... | collective-permute-start | bytes 98312 | tf_op jit(solution)/shard_map/while/body/eval_jaxpr/ppermute | solution.py:20
  74.1 6.7 %collective-permute-start = (f32[2,1,32,128]{3,2,1,0:T(8,128)S(1)}, f32[2,1,32,128]{3,2,1,0:T(8,128)S(1)}, u32[]{:S(2)}, u32[]{:S(2)}) collective-permute-start(f32[2,1,32,128]{3,2,1,0:T(8,128)S(1)} %get-tuple-element.225), channel_id=1, source_target_pairs={{8,0},{16,8},{24,16},{32,24},{40,32},{48,40},{56,48},{64,56},{72,6... | collective-permute-start | bytes 98312 | tf_op jit(solution)/shard_map/while/body/eval_jaxpr/ppermute | solution.py:23
  75.4 6.4 %collective-permute-start.1 = (f32[2,1,32,128]{3,2,1,0:T(8,128)S(1)}, f32[2,1,32,128]{3,2,1,0:T(8,128)S(1)}, u32[]{:S(2)}, u32[]{:S(2)}) collective-permute-start(f32[2,1,32,128]{3,2,1,0:T(8,128)S(1)} %get-tuple-element.226), channel_id=1, source_target_pairs={{0,8},{8,16},{16,24},{24,32},{32,40},{40,48},{48,56},{56,64},{64,7... | collective-permute-start | bytes 98312 | tf_op jit(solution)/shard_map/while/body/eval_jaxpr/ppermute | solution.py:20
  82.2 6.5 %collective-permute-start = (f32[2,1,32,128]{3,2,1,0:T(8,128)S(1)}, f32[2,1,32,128]{3,2,1,0:T(8,128)S(1)}, u32[]{:S(2)}, u32[]{:S(2)}) collective-permute-start(f32[2,1,32,128]{3,2,1,0:T(8,128)S(1)} %get-tuple-element.225), channel_id=1, source_target_pairs={{8,0},{16,8},{24,16},{32,24},{40,32},{48,40},{56,48},{64,56},{72,6... | collective-permute-start | bytes 98312 | tf_op jit(solution)/shard_map/while/body/eval_jaxpr/ppermute | solution.py:23
  83.5 6.2 %collective-permute-start.1 = (f32[2,1,32,128]{3,2,1,0:T(8,128)S(1)}, f32[2,1,32,128]{3,2,1,0:T(8,128)S(1)}, u32[]{:S(2)}, u32[]{:S(2)}) collective-permute-start(f32[2,1,32,128]{3,2,1,0:T(8,128)S(1)} %get-tuple-element.226), channel_id=1, source_target_pairs={{0,8},{8,16},{16,24},{24,32},{32,40},{40,48},{48,56},{56,64},{64,7... | collective-permute-start | bytes 98312 | tf_op jit(solution)/shard_map/while/body/eval_jaxpr/ppermute | solution.py:20
  90.2 7.9 %collective-permute-start = (f32[2,1,32,128]{3,2,1,0:T(8,128)S(1)}, f32[2,1,32,128]{3,2,1,0:T(8,128)S(1)}, u32[]{:S(2)}, u32[]{:S(2)}) collective-permute-start(f32[2,1,32,128]{3,2,1,0:T(8,128)S(1)} %get-tuple-element.225), channel_id=1, source_target_pairs={{8,0},{16,8},{24,16},{32,24},{40,32},{48,40},{56,48},{64,56},{72,6... | collective-permute-start | bytes 98312 | tf_op jit(solution)/shard_map/while/body/eval_jaxpr/ppermute | solution.py:23
  91.5 7.5 %collective-permute-start.1 = (f32[2,1,32,128]{3,2,1,0:T(8,128)S(1)}, f32[2,1,32,128]{3,2,1,0:T(8,128)S(1)}, u32[]{:S(2)}, u32[]{:S(2)}) collective-permute-start(f32[2,1,32,128]{3,2,1,0:T(8,128)S(1)} %get-tuple-element.226), channel_id=1, source_target_pairs={{0,8},{8,16},{16,24},{24,32},{32,40},{40,48},{48,56},{56,64},{64,7... | collective-permute-start | bytes 98312 | tf_op jit(solution)/shard_map/while/body/eval_jaxpr/ppermute | solution.py:20
  100.3 29.5 %all-to-all-start = ((f32[2,5,32,128]{3,0,1,2:T(2,128)}), f32[2,5,32,128]{3,0,1,2:T(2,128)S(1)}, u32[]{:S(2)}, u32[]{:S(2)}) async-start(f32[2,5,32,128]{3,0,1,2:T(2,128)} %copy.27), calls=%async_computation | async-start | bytes 327680 | tf_op jit(solution)/shard_map/all_to_all | solution.py:89
  129.8 0.7 copy-start
where the time goes:
time: 401 us; the launch traced here: 400 us
  blocking collectives  236 us (59%)
  starting transfers between devices  99.1 us (25%)
  other arithmetic  36.1 us (9%)
  waiting for transfers between devices  20.1 us (5%)
  local copies, waits for them, and re-layouts  7.41 us (2%)
    pmax x1, blocking collectives, body(): top_score = lax.pmax(local_top, ('space', 'sta'))  141 us
    psum x1, blocking collectives, body(): mass_sum = lax.psum(jnp.sum(cell_weights, 1), ('space', 'sta'))  94.4 us
    ppermute x12, starting transfers between devices, extended_2(): lax.ppermute(lax.slice_in_dim(block, block.shape[dim] - width, None, axis...  62.9 us
    all_to_all x1, starting transfers between devices, body(): lax.all_to_all(tables, 'sta', split_axis=2, concat_axis=0, tiled=True)  20.7 us
    ppermute x12, starting transfers between devices, extended_2(): lax.ppermute(lax.slice_in_dim(block, 0, width, axis=dim), axis, backward)  15.5 us
    reduce_sum x8, other arithmetic, misfit_block(): return jnp.sum(observed[:, :, None] * deviation * deviation, 1)  14 us
    ppermute x12, waiting for transfers between devices, extended_2(): lax.ppermute(lax.slice_in_dim(block, block.shape[dim] - width, None, axis...  11.5 us
    reduce_sum x8, other arithmetic, misfit_block(): jnp.sum(observed[:, :, None] * residual, 1) / pick_count[:, None]  9.54 us
  transfers between devices with their start and end apart: 25, of which 13 were waited for; matrix products, arithmetic and copies ran while one was open for 0% of the time, Pallas kernels for 0%

commit v1 on v0

--- a/solution.py
+++ b/solution.py
@@ -1,15 +1,113 @@
 import jax
 import jax.numpy as jnp
 from jax import lax
+from jax.experimental import pallas as pl
+from jax.experimental.pallas import tpu as pltpu
 from jax.sharding import PartitionSpec as P
 
 ROUNDS = 12
-
 
 BIG = 1000000.0
 pick_sigma = 0.25
 grid_step = 1.0
 block_events = 32
+NEAR = 2
+
+
+def merge_softmax_stats(top, mass, slots, count):
+    best = top
+    for k in range(count):
+        best = jnp.maximum(best, slots[k, 0:2])
+    total = mass * jnp.exp(top - best)
+    for k in range(count):
+        total = total + slots[k, 2:4] * jnp.exp(slots[k, 0:2] - best)
+    return best, total
+
+
+def stats_kernel(local_ref, out_ref, first, second, mid, send_sem, recv_sem):
+    space = lax.axis_index("space")
+    sta = lax.axis_index("sta")
+    stas = lax.axis_size("sta")
+    lines = lax.axis_size("space") // NEAR
+    line = space // NEAR
+    member = (space % NEAR) * stas + sta
+    members = NEAR * stas
+
+    def member_id(k):
+        other = (member + k) % members
+        return {"space": line * NEAR + other // stas, "sta": other % stas}
+
+    def line_id(k):
+        other = (line + k) % lines
+        return {"space": other * NEAR + space % NEAR, "sta": sta}
+
+    barrier = pltpu.get_barrier_semaphore()
+
+    def greet(ids, count):
+        def one(k, carry):
+            pl.semaphore_signal(barrier, inc=1, device_id=ids(k), device_id_type=pl.DeviceIdType.MESH)
+            return carry
+
+        lax.fori_loop(1, count, one, 0)
+
+    greet(member_id, members)
+    greet(line_id, lines)
+    pl.semaphore_wait(barrier, members + lines - 2)
+
+    def exchange(src, slots, ids, count, phase):
+        def copy(k):
+            return pltpu.make_async_remote_copy(
+                src_ref=src,
+                dst_ref=slots.at[k - 1],
+                send_sem=send_sem.at[phase, k - 1],
+                recv_sem=recv_sem.at[phase, k - 1],
+                device_id=ids(k),
+                device_id_type=pl.DeviceIdType.MESH,
+            )
+
+        def start(k, carry):
+            copy(k).start()
+            return carry
+
+        def wait(k, carry):
+            copy(k).wait()
+            return carry
+
+        lax.fori_loop(1, count, start, 0)
+        lax.fori_loop(1, count, wait, 0)
+
+    exchange(local_ref, first, member_id, members, 0)
+    top, mass = merge_softmax_stats(local_ref[0:2], local_ref[2:4], first, members - 1)
+    mid[0:2] = top
+    mid[2:4] = mass
+    exchange(mid, second, line_id, lines, 1)
+    top, mass = merge_softmax_stats(top, mass, second, lines - 1)
+    out_ref[0:2] = top
+    out_ref[2:4] = mass
+
+
+def global_stats(top, mass):
+    events = top.shape[0]
+    local = jnp.concatenate([top.reshape(2, -1), mass.reshape(2, -1)], 0)
+    members = NEAR * lax.axis_size("sta")
+    lines = lax.axis_size("space") // NEAR
+    longest = max(members, lines)
+    out = pl.pallas_call(
+        stats_kernel,
+        out_shape=jax.ShapeDtypeStruct(local.shape, jnp.float32),
+        in_specs=[pl.BlockSpec(memory_space=pltpu.VMEM)],
+        out_specs=pl.BlockSpec(memory_space=pltpu.VMEM),
+        scratch_shapes=[
+            pltpu.VMEM((members - 1,) + local.shape, jnp.float32),
+            pltpu.VMEM((lines - 1,) + local.shape, jnp.float32),
+            pltpu.VMEM(local.shape, jnp.float32),
+            pltpu.SemaphoreType.DMA((2, longest)),
+            pltpu.SemaphoreType.DMA((2, longest)),
+        ],
+        compiler_params=pltpu.CompilerParams(collective_id=0, has_side_effects=True),
+        name="stats",
+    )(local)
+    return out[0:2].reshape(events), out[2:4].reshape(events)
 
 
 def extended_2(block, sides, width):
@@ -96,10 +194,10 @@
     )
     score = -0.5 * blocks.reshape(picks.shape[0], -1) / (pick_sigma * pick_sigma)
     local_top = jnp.max(score, 1)
-    top_score = lax.pmax(local_top, ("space", "sta"))
-    cell_weights = jnp.exp(score - top_score[:, None])
-    mass_sum = lax.psum(jnp.sum(cell_weights, 1), ("space", "sta"))
-    density = cell_weights / mass_sum[:, None]
+    cell_weights = jnp.exp(score - local_top[:, None])
+    top_score, mass_sum = global_stats(local_top, jnp.sum(cell_weights, 1))
+    scale = jnp.exp(local_top - top_score) / mass_sum
+    density = cell_weights * scale[:, None]
     density = density.reshape(picks.shape[0], refined.shape[1], refined.shape[2], refined.shape[3])
     return (refined, density)
 

time: 401 us -> 231 us (0.58)
  blocking collectives: 236 us -> 0 us
  Pallas kernels: 0 us -> 64.5 us
    pmax x1 -> x0, blocking collectives: 141 us -> none  [body(): top_score = lax.pmax(local_top, ('space', 'sta'))]
    psum x1 -> x0, blocking collectives: 94.4 us -> none  [body(): mass_sum = lax.psum(jnp.sum(cell_weights, 1), ('space', 'sta'))]
    pallas_call x0 -> x1, Pallas kernels: none -> 64.5 us  [global_stats(): pl.pallas_call(stats_kernel, out_shape=jax.ShapeDtypeStruct(local.shape,...]
where the time goes in v1:
time: 231 us; the launch traced here: 230 us
  starting transfers between devices  99.1 us (43%)
  Pallas kernels  64.5 us (28%)
  other arithmetic  36.5 us (16%)
  waiting for transfers between devices  20.1 us (9%)
  local copies, waits for them, and re-layouts  7.42 us (3%)
    pallas_call x1, Pallas kernels, global_stats(): pl.pallas_call(stats_kernel, out_shape=jax.ShapeDtypeStruct(local.shape,...  64.5 us
    ppermute x12, starting transfers between devices, extended_2(): lax.ppermute(lax.slice_in_dim(block, block.shape[dim] - width, None, axis...  62.9 us
    all_to_all x1, starting transfers between devices, body(): lax.all_to_all(tables, 'sta', split_axis=2, concat_axis=0, tiled=True)  20.7 us
    ppermute x12, starting transfers between devices, extended_2(): lax.ppermute(lax.slice_in_dim(block, 0, width, axis=dim), axis, backward)  15.5 us
    reduce_sum x8, other arithmetic, misfit_block(): return jnp.sum(observed[:, :, None] * deviation * deviation, 1)  14 us
    ppermute x12, waiting for transfers between devices, extended_2(): lax.ppermute(lax.slice_in_dim(block, block.shape[dim] - width, None, axis...  11.5 us
    reduce_sum x8, other arithmetic, misfit_block(): jnp.sum(observed[:, :, None] * residual, 1) / pick_count[:, None]  9.54 us
    all_to_all x1, waiting for transfers between devices, body(): lax.all_to_all(tables, 'sta', split_axis=2, concat_axis=0, tiled=True)  8.57 us
  transfers between devices with their start and end apart: 25, of which 13 were waited for; matrix products, arithmetic and copies ran while one was open for 0% of the time, Pallas kernels for 0%

profile of v1, /device:TPU:1, one launch (start us, length us, event | category | flops | bytes accessed | tf_op | source)
XLA Modules:
  0.0 229.6 jit_solution(10749405119259208712)
XLA Ops:
  1.5 1.5 select_reduce_fusion
  3.1 96.4 %while.22 = (s32[]{:T(128)}, f32[2,5,32,128]{3,2,1,0:T(8,128)S(1)}, pred[]{:T(512)}, pred[]{:T(512)}, f32[5,32,128]{2,1,0:T(8,128)S(1)}, /*index=5*/f32[1,5,32,128]{3,2,1,0:T(8,128)S(1)}, s32[]{:T(128)}) while((s32[]{:T(128)}, f32[2,5,32,128]{3,2,1,0:T(8,128)S(1)}, pred[]{:T(512)}, pred[]{:T(512)}, f32[5,32,128]{2,1,0:T(8,128)S(1)}, ...), condition=%wide.region_2.3_spmd, body=%wide.region_1.2_spmd.sunk | while | flops 1523749 | bytes 2244781 | solution.py:186
  3.1 1.3 collective-permute-start
  4.4 4.6 %collective-permute-start.1 = (f32[2,1,32,128]{3,2,1,0:T(8,128)S(1)}, f32[2,1,32,128]{3,2,1,0:T(8,128)S(1)}, u32[]{:S(2)}, u32[]{:S(2)}) collective-permute-start(f32[2,1,32,128]{3,2,1,0:T(8,128)S(1)} %get-tuple-element.226), channel_id=1, source_target_pairs={{0,8},{8,16},{16,24},{24,32},{32,40},{40,48},{48,56},{56,64},{64,7... | collective-permute-start | bytes 98312 | tf_op jit(solution)/shard_map/while/body/eval_jaxpr/ppermute | solution.py:118
  10.6 1.3 collective-permute-start
  11.9 4.9 %collective-permute-start.1 = (f32[2,1,32,128]{3,2,1,0:T(8,128)S(1)}, f32[2,1,32,128]{3,2,1,0:T(8,128)S(1)}, u32[]{:S(2)}, u32[]{:S(2)}) collective-permute-start(f32[2,1,32,128]{3,2,1,0:T(8,128)S(1)} %get-tuple-element.226), channel_id=1, source_target_pairs={{0,8},{8,16},{16,24},{24,32},{32,40},{40,48},{48,56},{56,64},{64,7... | collective-permute-start | bytes 98312 | tf_op jit(solution)/shard_map/while/body/eval_jaxpr/ppermute | solution.py:118
  18.2 1.3 collective-permute-start
  19.5 5.2 %collective-permute-start.1 = (f32[2,1,32,128]{3,2,1,0:T(8,128)S(1)}, f32[2,1,32,128]{3,2,1,0:T(8,128)S(1)}, u32[]{:S(2)}, u32[]{:S(2)}) collective-permute-start(f32[2,1,32,128]{3,2,1,0:T(8,128)S(1)} %get-tuple-element.226), channel_id=1, source_target_pairs={{0,8},{8,16},{16,24},{24,32},{32,40},{40,48},{48,56},{56,64},{64,7... | collective-permute-start | bytes 98312 | tf_op jit(solution)/shard_map/while/body/eval_jaxpr/ppermute | solution.py:118
  27.5 5.2 %collective-permute-start.1 = (f32[2,1,32,128]{3,2,1,0:T(8,128)S(1)}, f32[2,1,32,128]{3,2,1,0:T(8,128)S(1)}, u32[]{:S(2)}, u32[]{:S(2)}) collective-permute-start(f32[2,1,32,128]{3,2,1,0:T(8,128)S(1)} %get-tuple-element.226), channel_id=1, source_target_pairs={{0,8},{8,16},{16,24},{24,32},{32,40},{40,48},{48,56},{56,64},{64,7... | collective-permute-start | bytes 98312 | tf_op jit(solution)/shard_map/while/body/eval_jaxpr/ppermute | solution.py:118
  35.5 5.2 %collective-permute-start.1 = (f32[2,1,32,128]{3,2,1,0:T(8,128)S(1)}, f32[2,1,32,128]{3,2,1,0:T(8,128)S(1)}, u32[]{:S(2)}, u32[]{:S(2)}) collective-permute-start(f32[2,1,32,128]{3,2,1,0:T(8,128)S(1)} %get-tuple-element.226), channel_id=1, source_target_pairs={{0,8},{8,16},{16,24},{24,32},{32,40},{40,48},{48,56},{56,64},{64,7... | collective-permute-start | bytes 98312 | tf_op jit(solution)/shard_map/while/body/eval_jaxpr/ppermute | solution.py:118
  43.4 5.2 %collective-permute-start.1 = (f32[2,1,32,128]{3,2,1,0:T(8,128)S(1)}, f32[2,1,32,128]{3,2,1,0:T(8,128)S(1)}, u32[]{:S(2)}, u32[]{:S(2)}) collective-permute-start(f32[2,1,32,128]{3,2,1,0:T(8,128)S(1)} %get-tuple-element.226), channel_id=1, source_target_pairs={{0,8},{8,16},{16,24},{24,32},{32,40},{40,48},{48,56},{56,64},{64,7... | collective-permute-start | bytes 98312 | tf_op jit(solution)/shard_map/while/body/eval_jaxpr/ppermute | solution.py:118
  51.4 5.2 %collective-permute-start.1 = (f32[2,1,32,128]{3,2,1,0:T(8,128)S(1)}, f32[2,1,32,128]{3,2,1,0:T(8,128)S(1)}, u32[]{:S(2)}, u32[]{:S(2)}) collective-permute-start(f32[2,1,32,128]{3,2,1,0:T(8,128)S(1)} %get-tuple-element.226), channel_id=1, source_target_pairs={{0,8},{8,16},{16,24},{24,32},{32,40},{40,48},{48,56},{56,64},{64,7... | collective-permute-start | bytes 98312 | tf_op jit(solution)/shard_map/while/body/eval_jaxpr/ppermute | solution.py:118
  59.4 5.2 %collective-permute-start.1 = (f32[2,1,32,128]{3,2,1,0:T(8,128)S(1)}, f32[2,1,32,128]{3,2,1,0:T(8,128)S(1)}, u32[]{:S(2)}, u32[]{:S(2)}) collective-permute-start(f32[2,1,32,128]{3,2,1,0:T(8,128)S(1)} %get-tuple-element.226), channel_id=1, source_target_pairs={{0,8},{8,16},{16,24},{24,32},{32,40},{40,48},{48,56},{56,64},{64,7... | collective-permute-start | bytes 98312 | tf_op jit(solution)/shard_map/while/body/eval_jaxpr/ppermute | solution.py:118
  67.3 5.3 %collective-permute-start.1 = (f32[2,1,32,128]{3,2,1,0:T(8,128)S(1)}, f32[2,1,32,128]{3,2,1,0:T(8,128)S(1)}, u32[]{:S(2)}, u32[]{:S(2)}) collective-permute-start(f32[2,1,32,128]{3,2,1,0:T(8,128)S(1)} %get-tuple-element.226), channel_id=1, source_target_pairs={{0,8},{8,16},{16,24},{24,32},{32,40},{40,48},{48,56},{56,64},{64,7... | collective-permute-start | bytes 98312 | tf_op jit(solution)/shard_map/while/body/eval_jaxpr/ppermute | solution.py:118
  75.4 5.3 %collective-permute-start.1 = (f32[2,1,32,128]{3,2,1,0:T(8,128)S(1)}, f32[2,1,32,128]{3,2,1,0:T(8,128)S(1)}, u32[]{:S(2)}, u32[]{:S(2)}) collective-permute-start(f32[2,1,32,128]{3,2,1,0:T(8,128)S(1)} %get-tuple-element.226), channel_id=1, source_target_pairs={{0,8},{8,16},{16,24},{24,32},{32,40},{40,48},{48,56},{56,64},{64,7... | collective-permute-start | bytes 98312 | tf_op jit(solution)/shard_map/while/body/eval_jaxpr/ppermute | solution.py:118
  83.5 5.2 %collective-permute-start.1 = (f32[2,1,32,128]{3,2,1,0:T(8,128)S(1)}, f32[2,1,32,128]{3,2,1,0:T(8,128)S(1)}, u32[]{:S(2)}, u32[]{:S(2)}) collective-permute-start(f32[2,1,32,128]{3,2,1,0:T(8,128)S(1)} %get-tuple-element.226), channel_id=1, source_target_pairs={{0,8},{8,16},{16,24},{24,32},{32,40},{40,48},{48,56},{56,64},{64,7... | collective-permute-start | bytes 98312 | tf_op jit(solution)/shard_map/while/body/eval_jaxpr/ppermute | solution.py:118
  91.5 6.5 %collective-permute-start.1 = (f32[2,1,32,128]{3,2,1,0:T(8,128)S(1)}, f32[2,1,32,128]{3,2,1,0:T(8,128)S(1)}, u32[]{:S(2)}, u32[]{:S(2)}) collective-permute-start(f32[2,1,32,128]{3,2,1,0:T(8,128)S(1)} %get-tuple-element.226), channel_id=1, source_target_pairs={{0,8},{8,16},{16,24},{24,32},{32,40},{40,48},{48,56},{56,64},{64,7... | collective-permute-start | bytes 98312 | tf_op jit(solution)/shard_map/while/body/eval_jaxpr/ppermute | solution.py:118
  100.3 20.7 %all-to-all-start = ((f32[2,5,32,128]{3,0,1,2:T(2,128)}), f32[2,5,32,128]{3,0,1,2:T(2,128)S(1)}, u32[]{:S(2)}, u32[]{:S(2)}) async-start(f32[2,5,32,128]{3,0,1,2:T(2,128)} %copy.27), calls=%async_computation | async-start | bytes 327680 | tf_op jit(solution)/shard_map/all_to_all | solution.py:187
  121.2 8.6 %all-to-all-done = f32[2,5,32,128]{3,0,1,2:T(2,128)S(1)} async-done(((f32[2,5,32,128]{3,0,1,2:T(2,128)}), f32[2,5,32,128]{3,0,1,2:T(2,128)S(1)}, u32[]{:S(2)}, u32[]{:S(2)}) %all-to-all-start) | async-done | bytes 163872 | tf_op jit(solution)/shard_map/all_to_all | solution.py:187
  130.4 26.5 %while.23 = (s32[]{:T(128)}, f32[8,32,2560]{2,1,0:T(8,128)S(1)}, f32[8,32,16]{1,0,2:T(8,128)S(1)}, f32[8,32,16]{1,0,2:T(8,128)S(1)}, f32[16,5,4,128]{3,2,1,0:T(4...) while((s32[]{:T(128)}, f32[8,32,2560]{2,1,0:T(8,128)S(1)}, f32[8,32,16]{1,0,2:T(8,128)S(1)}, ...), condition=%wide.wide.region_7.8_spmd, body=%wide.wide.region_3.7_spmd.sunk | while | flops 10404322 | bytes 2648417 | solution.py:191
  131.9 1.8 fusion.19
  135.3 1.8 fusion.19
  138.6 1.8 fusion.19
  141.9 1.8 fusion.19
  145.2 1.8 fusion.19
  148.5 1.8 fusion.19
  151.8 1.8 fusion.19
  155.1 1.8 fusion.19
  157.2 2.0 exponential_reduce_fusion
  160.0 64.5 %stats.1 = f32[4,128]{1,0:T(4,128)} custom-call(f32[4,128]{1,0:T(4,128)} %pad_maximum_fusion.local_ref), custom_call_target="tpu_custom_call" | custom-call | tf_op jit(solution)/shard_map/stats/pallas_call | solution.py:95
  224.5 2.8 %div.32 = f32[256,5,4,128]{3,2,1,0:T(4,128)S(1)} reshape(f32[8,32,2560]{2,1,0:T(8,128)} %get-tuple-element.130) | data formatting | bytes 5242880 | tf_op jit(solution)/shard_map/div | solution.py:195
  227.3 2.3 exponential_multiply_fusion
  (184 shorter events, 44.4 us)
Async XLA Ops:
  3.1 117.9 %copy-start.2 = (s32[256,16]{0,1:T(8,128)S(1)}, s32[256,16]{0,1:T(8,128)}, u32[]{:S(2)}) copy-start(s32[256,16]{0,1:T(8,128)} %param.13) | copy-start | bytes 49156
  3.1 118.0 %copy-start.1 = (f32[256,16]{0,1:T(8,128)S(1)}, f32[256,16]{0,1:T(8,128)}, u32[]{:S(2)}) copy-start(f32[256,16]{0,1:T(8,128)} %param.12) | copy-start | bytes 49156
  3.1 6.0 %collective-permute-start = (f32[2,1,32,128]{3,2,1,0:T(8,128)S(1)}, f32[2,1,32,128]{3,2,1,0:T(8,128)S(1)}, u32[]{:S(2)}, u32[]{:S(2)}) collective-permute-start(f32[2,1,32,128]{3,2,1,0:T(8,128)S(1)} %get-tuple-element.225), channel_id=1, source_target_pairs={{8,0},{16,8},{24,16},{32,24},{40,32},{48,40},{56,48},{64,56},{72,6... | collective-permute-start | bytes 98312 | tf_op jit(solution)/shard_map/while/body/eval_jaxpr/ppermute | solution.py:121
  4.4 5.7 %collective-permute-start.1 = (f32[2,1,32,128]{3,2,1,0:T(8,128)S(1)}, f32[2,1,32,128]{3,2,1,0:T(8,128)S(1)}, u32[]{:S(2)}, u32[]{:S(2)}) collective-permute-start(f32[2,1,32,128]{3,2,1,0:T(8,128)S(1)} %get-tuple-element.226), channel_id=1, source_target_pairs={{0,8},{8,16},{16,24},{24,32},{32,40},{40,48},{48,56},{56,64},{64,7... | collective-permute-start | bytes 98312 | tf_op jit(solution)/shard_map/while/body/eval_jaxpr/ppermute | solution.py:118
  10.6 6.2 %collective-permute-start = (f32[2,1,32,128]{3,2,1,0:T(8,128)S(1)}, f32[2,1,32,128]{3,2,1,0:T(8,128)S(1)}, u32[]{:S(2)}, u32[]{:S(2)}) collective-permute-start(f32[2,1,32,128]{3,2,1,0:T(8,128)S(1)} %get-tuple-element.225), channel_id=1, source_target_pairs={{8,0},{16,8},{24,16},{32,24},{40,32},{48,40},{56,48},{64,56},{72,6... | collective-permute-start | bytes 98312 | tf_op jit(solution)/shard_map/while/body/eval_jaxpr/ppermute | solution.py:121
  11.9 5.9 %collective-permute-start.1 = (f32[2,1,32,128]{3,2,1,0:T(8,128)S(1)}, f32[2,1,32,128]{3,2,1,0:T(8,128)S(1)}, u32[]{:S(2)}, u32[]{:S(2)}) collective-permute-start(f32[2,1,32,128]{3,2,1,0:T(8,128)S(1)} %get-tuple-element.226), channel_id=1, source_target_pairs={{0,8},{8,16},{16,24},{24,32},{32,40},{40,48},{48,56},{56,64},{64,7... | collective-permute-start | bytes 98312 | tf_op jit(solution)/shard_map/while/body/eval_jaxpr/ppermute | solution.py:118
  18.2 6.5 %collective-permute-start = (f32[2,1,32,128]{3,2,1,0:T(8,128)S(1)}, f32[2,1,32,128]{3,2,1,0:T(8,128)S(1)}, u32[]{:S(2)}, u32[]{:S(2)}) collective-permute-start(f32[2,1,32,128]{3,2,1,0:T(8,128)S(1)} %get-tuple-element.225), channel_id=1, source_target_pairs={{8,0},{16,8},{24,16},{32,24},{40,32},{48,40},{56,48},{64,56},{72,6... | collective-permute-start | bytes 98312 | tf_op jit(solution)/shard_map/while/body/eval_jaxpr/ppermute | solution.py:121
  19.5 6.2 %collective-permute-start.1 = (f32[2,1,32,128]{3,2,1,0:T(8,128)S(1)}, f32[2,1,32,128]{3,2,1,0:T(8,128)S(1)}, u32[]{:S(2)}, u32[]{:S(2)}) collective-permute-start(f32[2,1,32,128]{3,2,1,0:T(8,128)S(1)} %get-tuple-element.226), channel_id=1, source_target_pairs={{0,8},{8,16},{16,24},{24,32},{32,40},{40,48},{48,56},{56,64},{64,7... | collective-permute-start | bytes 98312 | tf_op jit(solution)/shard_map/while/body/eval_jaxpr/ppermute | solution.py:118
  26.2 6.5 %collective-permute-start = (f32[2,1,32,128]{3,2,1,0:T(8,128)S(1)}, f32[2,1,32,128]{3,2,1,0:T(8,128)S(1)}, u32[]{:S(2)}, u32[]{:S(2)}) collective-permute-start(f32[2,1,32,128]{3,2,1,0:T(8,128)S(1)} %get-tuple-element.225), channel_id=1, source_target_pairs={{8,0},{16,8},{24,16},{32,24},{40,32},{48,40},{56,48},{64,56},{72,6... | collective-permute-start | bytes 98312 | tf_op jit(solution)/shard_map/while/body/eval_jaxpr/ppermute | solution.py:121
  27.5 6.2 %collective-permute-start.1 = (f32[2,1,32,128]{3,2,1,0:T(8,128)S(1)}, f32[2,1,32,128]{3,2,1,0:T(8,128)S(1)}, u32[]{:S(2)}, u32[]{:S(2)}) collective-permute-start(f32[2,1,32,128]{3,2,1,0:T(8,128)S(1)} %get-tuple-element.226), channel_id=1, source_target_pairs={{0,8},{8,16},{16,24},{24,32},{32,40},{40,48},{48,56},{56,64},{64,7... | collective-permute-start | bytes 98312 | tf_op jit(solution)/shard_map/while/body/eval_jaxpr/ppermute | solution.py:118
  34.2 6.5 %collective-permute-start = (f32[2,1,32,128]{3,2,1,0:T(8,128)S(1)}, f32[2,1,32,128]{3,2,1,0:T(8,128)S(1)}, u32[]{:S(2)}, u32[]{:S(2)}) collective-permute-start(f32[2,1,32,128]{3,2,1,0:T(8,128)S(1)} %get-tuple-element.225), channel_id=1, source_target_pairs={{8,0},{16,8},{24,16},{32,24},{40,32},{48,40},{56,48},{64,56},{72,6... | collective-permute-start | bytes 98312 | tf_op jit(solution)/shard_map/while/body/eval_jaxpr/ppermute | solution.py:121
  35.5 6.2 %collective-permute-start.1 = (f32[2,1,32,128]{3,2,1,0:T(8,128)S(1)}, f32[2,1,32,128]{3,2,1,0:T(8,128)S(1)}, u32[]{:S(2)}, u32[]{:S(2)}) collective-permute-start(f32[2,1,32,128]{3,2,1,0:T(8,128)S(1)} %get-tuple-element.226), channel_id=1, source_target_pairs={{0,8},{8,16},{16,24},{24,32},{32,40},{40,48},{48,56},{56,64},{64,7... | collective-permute-start | bytes 98312 | tf_op jit(solution)/shard_map/while/body/eval_jaxpr/ppermute | solution.py:118
  42.1 6.5 %collective-permute-start = (f32[2,1,32,128]{3,2,1,0:T(8,128)S(1)}, f32[2,1,32,128]{3,2,1,0:T(8,128)S(1)}, u32[]{:S(2)}, u32[]{:S(2)}) collective-permute-start(f32[2,1,32,128]{3,2,1,0:T(8,128)S(1)} %get-tuple-element.225), channel_id=1, source_target_pairs={{8,0},{16,8},{24,16},{32,24},{40,32},{48,40},{56,48},{64,56},{72,6... | collective-permute-start | bytes 98312 | tf_op jit(solution)/shard_map/while/body/eval_jaxpr/ppermute | solution.py:121
  43.4 6.2 %collective-permute-start.1 = (f32[2,1,32,128]{3,2,1,0:T(8,128)S(1)}, f32[2,1,32,128]{3,2,1,0:T(8,128)S(1)}, u32[]{:S(2)}, u32[]{:S(2)}) collective-permute-start(f32[2,1,32,128]{3,2,1,0:T(8,128)S(1)} %get-tuple-element.226), channel_id=1, source_target_pairs={{0,8},{8,16},{16,24},{24,32},{32,40},{40,48},{48,56},{56,64},{64,7... | collective-permute-start | bytes 98312 | tf_op jit(solution)/shard_map/while/body/eval_jaxpr/ppermute | solution.py:118
  50.1 6.5 %collective-permute-start = (f32[2,1,32,128]{3,2,1,0:T(8,128)S(1)}, f32[2,1,32,128]{3,2,1,0:T(8,128)S(1)}, u32[]{:S(2)}, u32[]{:S(2)}) collective-permute-start(f32[2,1,32,128]{3,2,1,0:T(8,128)S(1)} %get-tuple-element.225), channel_id=1, source_target_pairs={{8,0},{16,8},{24,16},{32,24},{40,32},{48,40},{56,48},{64,56},{72,6... | collective-permute-start | bytes 98312 | tf_op jit(solution)/shard_map/while/body/eval_jaxpr/ppermute | solution.py:121
  51.4 6.2 %collective-permute-start.1 = (f32[2,1,32,128]{3,2,1,0:T(8,128)S(1)}, f32[2,1,32,128]{3,2,1,0:T(8,128)S(1)}, u32[]{:S(2)}, u32[]{:S(2)}) collective-permute-start(f32[2,1,32,128]{3,2,1,0:T(8,128)S(1)} %get-tuple-element.226), channel_id=1, source_target_pairs={{0,8},{8,16},{16,24},{24,32},{32,40},{40,48},{48,56},{56,64},{64,7... | collective-permute-start | bytes 98312 | tf_op jit(solution)/shard_map/while/body/eval_jaxpr/ppermute | solution.py:118
  58.1 6.5 %collective-permute-start = (f32[2,1,32,128]{3,2,1,0:T(8,128)S(1)}, f32[2,1,32,128]{3,2,1,0:T(8,128)S(1)}, u32[]{:S(2)}, u32[]{:S(2)}) collective-permute-start(f32[2,1,32,128]{3,2,1,0:T(8,128)S(1)} %get-tuple-element.225), channel_id=1, source_target_pairs={{8,0},{16,8},{24,16},{32,24},{40,32},{48,40},{56,48},{64,56},{72,6... | collective-permute-start | bytes 98312 | tf_op jit(solution)/shard_map/while/body/eval_jaxpr/ppermute | solution.py:121
  59.4 6.2 %collective-permute-start.1 = (f32[2,1,32,128]{3,2,1,0:T(8,128)S(1)}, f32[2,1,32,128]{3,2,1,0:T(8,128)S(1)}, u32[]{:S(2)}, u32[]{:S(2)}) collective-permute-start(f32[2,1,32,128]{3,2,1,0:T(8,128)S(1)} %get-tuple-element.226), channel_id=1, source_target_pairs={{0,8},{8,16},{16,24},{24,32},{32,40},{40,48},{48,56},{56,64},{64,7... | collective-permute-start | bytes 98312 | tf_op jit(solution)/shard_map/while/body/eval_jaxpr/ppermute | solution.py:118
  66.0 6.6 %collective-permute-start = (f32[2,1,32,128]{3,2,1,0:T(8,128)S(1)}, f32[2,1,32,128]{3,2,1,0:T(8,128)S(1)}, u32[]{:S(2)}, u32[]{:S(2)}) collective-permute-start(f32[2,1,32,128]{3,2,1,0:T(8,128)S(1)} %get-tuple-element.225), channel_id=1, source_target_pairs={{8,0},{16,8},{24,16},{32,24},{40,32},{48,40},{56,48},{64,56},{72,6... | collective-permute-start | bytes 98312 | tf_op jit(solution)/shard_map/while/body/eval_jaxpr/ppermute | solution.py:121
  67.3 6.3 %collective-permute-start.1 = (f32[2,1,32,128]{3,2,1,0:T(8,128)S(1)}, f32[2,1,32,128]{3,2,1,0:T(8,128)S(1)}, u32[]{:S(2)}, u32[]{:S(2)}) collective-permute-start(f32[2,1,32,128]{3,2,1,0:T(8,128)S(1)} %get-tuple-element.226), channel_id=1, source_target_pairs={{0,8},{8,16},{16,24},{24,32},{32,40},{40,48},{48,56},{56,64},{64,7... | collective-permute-start | bytes 98312 | tf_op jit(solution)/shard_map/while/body/eval_jaxpr/ppermute | solution.py:118
  74.1 6.7 %collective-permute-start = (f32[2,1,32,128]{3,2,1,0:T(8,128)S(1)}, f32[2,1,32,128]{3,2,1,0:T(8,128)S(1)}, u32[]{:S(2)}, u32[]{:S(2)}) collective-permute-start(f32[2,1,32,128]{3,2,1,0:T(8,128)S(1)} %get-tuple-element.225), channel_id=1, source_target_pairs={{8,0},{16,8},{24,16},{32,24},{40,32},{48,40},{56,48},{64,56},{72,6... | collective-permute-start | bytes 98312 | tf_op jit(solution)/shard_map/while/body/eval_jaxpr/ppermute | solution.py:121
  75.4 6.4 %collective-permute-start.1 = (f32[2,1,32,128]{3,2,1,0:T(8,128)S(1)}, f32[2,1,32,128]{3,2,1,0:T(8,128)S(1)}, u32[]{:S(2)}, u32[]{:S(2)}) collective-permute-start(f32[2,1,32,128]{3,2,1,0:T(8,128)S(1)} %get-tuple-element.226), channel_id=1, source_target_pairs={{0,8},{8,16},{16,24},{24,32},{32,40},{40,48},{48,56},{56,64},{64,7... | collective-permute-start | bytes 98312 | tf_op jit(solution)/shard_map/while/body/eval_jaxpr/ppermute | solution.py:118
  82.2 6.5 %collective-permute-start = (f32[2,1,32,128]{3,2,1,0:T(8,128)S(1)}, f32[2,1,32,128]{3,2,1,0:T(8,128)S(1)}, u32[]{:S(2)}, u32[]{:S(2)}) collective-permute-start(f32[2,1,32,128]{3,2,1,0:T(8,128)S(1)} %get-tuple-element.225), channel_id=1, source_target_pairs={{8,0},{16,8},{24,16},{32,24},{40,32},{48,40},{56,48},{64,56},{72,6... | collective-permute-start | bytes 98312 | tf_op jit(solution)/shard_map/while/body/eval_jaxpr/ppermute | solution.py:121
  83.5 6.2 %collective-permute-start.1 = (f32[2,1,32,128]{3,2,1,0:T(8,128)S(1)}, f32[2,1,32,128]{3,2,1,0:T(8,128)S(1)}, u32[]{:S(2)}, u32[]{:S(2)}) collective-permute-start(f32[2,1,32,128]{3,2,1,0:T(8,128)S(1)} %get-tuple-element.226), channel_id=1, source_target_pairs={{0,8},{8,16},{16,24},{24,32},{32,40},{40,48},{48,56},{56,64},{64,7... | collective-permute-start | bytes 98312 | tf_op jit(solution)/shard_map/while/body/eval_jaxpr/ppermute | solution.py:118
  90.2 7.9 %collective-permute-start = (f32[2,1,32,128]{3,2,1,0:T(8,128)S(1)}, f32[2,1,32,128]{3,2,1,0:T(8,128)S(1)}, u32[]{:S(2)}, u32[]{:S(2)}) collective-permute-start(f32[2,1,32,128]{3,2,1,0:T(8,128)S(1)} %get-tuple-element.225), channel_id=1, source_target_pairs={{8,0},{16,8},{24,16},{32,24},{40,32},{48,40},{56,48},{64,56},{72,6... | collective-permute-start | bytes 98312 | tf_op jit(solution)/shard_map/while/body/eval_jaxpr/ppermute | solution.py:121
  91.5 7.5 %collective-permute-start.1 = (f32[2,1,32,128]{3,2,1,0:T(8,128)S(1)}, f32[2,1,32,128]{3,2,1,0:T(8,128)S(1)}, u32[]{:S(2)}, u32[]{:S(2)}) collective-permute-start(f32[2,1,32,128]{3,2,1,0:T(8,128)S(1)} %get-tuple-element.226), channel_id=1, source_target_pairs={{0,8},{8,16},{16,24},{24,32},{32,40},{40,48},{48,56},{56,64},{64,7... | collective-permute-start | bytes 98312 | tf_op jit(solution)/shard_map/while/body/eval_jaxpr/ppermute | solution.py:118
  100.3 29.5 %all-to-all-start = ((f32[2,5,32,128]{3,0,1,2:T(2,128)}), f32[2,5,32,128]{3,0,1,2:T(2,128)S(1)}, u32[]{:S(2)}, u32[]{:S(2)}) async-start(f32[2,5,32,128]{3,0,1,2:T(2,128)} %copy.27), calls=%async_computation | async-start | bytes 327680 | tf_op jit(solution)/shard_map/all_to_all | solution.py:187
  129.8 0.7 copy-start
  224.5 2.9 %copy-start.3 = (f32[4,128]{1,0:T(4,128)S(1)}, f32[4,128]{1,0:T(4,128)}, u32[]{:S(2)}) copy-start(f32[4,128]{1,0:T(4,128)} %stats.1) | copy-start | bytes 6148

commit v2 on v1

--- a/solution.py
+++ b/solution.py
@@ -110,53 +110,351 @@
     return out[0:2].reshape(events), out[2:4].reshape(events)
 
 
-def extended_2(block, sides, width):
-    for axis, dim in sides:
-        count = lax.axis_size(axis)
-        forward = [(i, i + 1) for i in range(count - 1)]
-        backward = [(target, source) for source, target in forward]
-        low = lax.ppermute(
-            lax.slice_in_dim(block, block.shape[dim] - width, None, axis=dim), axis, forward
-        )
-        high = lax.ppermute(lax.slice_in_dim(block, 0, width, axis=dim), axis, backward)
-        block = jnp.concatenate([low, block, high], axis=dim)
-    return block
+HALO = 4
+PAD = 8
+
+
+def speed_kernel(table_ref, map_ref, out_ref):
+    for plane in range(map_ref.shape[0]):
+        index = map_ref[plane]
+        table = jnp.broadcast_to(table_ref[...], index.shape)
+        out_ref[plane] = grid_step * jnp.take_along_axis(table, index, axis=1)
+
+
+def speed_of(model_map, slowness):
+    lanes = model_map.shape[-1]
+    table = jnp.pad(slowness, (0, lanes - slowness.shape[0])).reshape(1, lanes)
+    return pl.pallas_call(
+        speed_kernel,
+        out_shape=jax.ShapeDtypeStruct(model_map.shape, jnp.float32),
+        in_specs=[pl.BlockSpec(memory_space=pltpu.VMEM)] * 2,
+        out_specs=pl.BlockSpec(memory_space=pltpu.VMEM),
+        name="speed",
+    )(table, model_map)
 
 
 def godunov(near_one, near_two, near_three, speed):
-    lowest = jnp.minimum(jnp.minimum(near_one, near_two), near_three)
-    highest = jnp.maximum(jnp.maximum(near_one, near_two), near_three)
-    middle = jnp.maximum(
-        jnp.minimum(near_one, near_two), jnp.minimum(jnp.maximum(near_one, near_two), near_three)
-    )
+    small = jnp.minimum(near_one, near_two)
+    large = jnp.maximum(near_one, near_two)
+    lowest = jnp.minimum(small, near_three)
+    highest = jnp.maximum(large, near_three)
+    middle = jnp.maximum(small, jnp.minimum(large, near_three))
     gap_mid = middle - lowest
     gap_high = highest - lowest
-    two_sided = 0.5 * (
-        gap_mid + jnp.sqrt(jnp.maximum(2.0 * speed * speed - gap_mid * gap_mid, 0.0))
-    )
-    gap_sum = gap_mid + gap_high
-    squares = gap_mid * gap_mid + gap_high * gap_high - speed * speed
-    three_sided = (gap_sum + jnp.sqrt(jnp.maximum(gap_sum * gap_sum - 3.0 * squares, 0.0))) / 3.0
-    increase = jnp.where(
-        speed <= gap_mid, speed, jnp.where(two_sided <= gap_high, two_sided, three_sided)
-    )
-    return lowest + increase
-
-
-def relax(extended, speed):
-    centre = extended[:, 1:-1]
-    along_x = jnp.minimum(extended[:, :-2], extended[:, 2:])
-    padded = jnp.pad(centre, ((0, 0), (0, 0), (1, 1), (1, 1)), constant_values=BIG)
-    along_y = jnp.minimum(padded[:, :, :-2, 1:-1], padded[:, :, 2:, 1:-1])
-    along_z = jnp.minimum(padded[:, :, 1:-1, :-2], padded[:, :, 1:-1, 2:])
-    return jnp.minimum(centre, godunov(along_x, along_y, along_z, speed[None]))
-
-
-def close_rims(extended, rim_width, at_lower, at_upper):
-    cell_count = extended.shape[1]
-    position = lax.broadcasted_iota(jnp.int32, (1, cell_count, 1, 1), 1)
-    outside = (position < rim_width) & at_lower | (position >= cell_count - rim_width) & at_upper
-    return jnp.where(outside, BIG, extended)
+    spread = highest - middle
+    square = speed * speed
+    mid_square = gap_mid * gap_mid
+    reach = gap_high * gap_high + spread * spread
+    two = square <= reach
+    inner = jnp.where(two, 2.0 * square, 3.0 * square - reach) - mid_square
+    root = jnp.sqrt(jnp.maximum(inner, 0.0))
+    base = gap_mid + jnp.where(two, 0.0, gap_high)
+    steep = (base + root) * jnp.where(two, 0.5, 1.0 / 3.0)
+    return lowest + jnp.where(speed <= gap_mid, speed, steep)
+
+
+def travel_kernel(
+    times_ref,
+    speed_ref,
+    refined_ref,
+    tab,
+    spd,
+    swap_in,
+    swap_speed,
+    halo_in,
+    halo_speed,
+    edge_out,
+    stage,
+    arrived,
+    start_send,
+    start_recv,
+    halo_send,
+    halo_recv,
+    all_send,
+    all_recv,
+):
+    space = lax.axis_index("space")
+    sta = lax.axis_index("sta")
+    stas = lax.axis_size("sta")
+    lines = lax.axis_size("space") // NEAR
+    line = space // NEAR
+    half = space % NEAR
+    depth, rows, lanes = speed_ref.shape
+    own = NEAR * depth
+    count = own + 2 * HALO
+    piece = stage.shape[2]
+    member = half * stas + sta
+    members = NEAR * stas
+    station = NEAR * sta + half
+    inside = pl.ds(PAD, rows)
+    mesh_id = pl.DeviceIdType.MESH
+
+    def at(other_line, other_half):
+        return {"space": ((other_line + lines) % lines) * NEAR + other_half, "sta": sta}
+
+    def member_at(other):
+        return {"space": line * NEAR + other // stas, "sta": other % stas}
+
+    barrier = pltpu.get_barrier_semaphore()
+
+    def greet(j, carry):
+        pl.semaphore_signal(
+            barrier, inc=1, device_id=member_at((member + j) % members), device_id_type=mesh_id
+        )
+        return carry
+
+    for other_line in (line - 1, line + 1):
+        for other_half in range(NEAR):
+            pl.semaphore_signal(
+                barrier, inc=1, device_id=at(other_line, other_half), device_id_type=mesh_id
+            )
+    lax.fori_loop(1, members, greet, 0)
+
+    rim = jnp.full((PAD, lanes), BIG, jnp.float32)
+
+    def rims(plane, carry):
+        for side in range(2):
+            tab[side, plane, pl.ds(0, PAD)] = rim
+            tab[side, plane, pl.ds(PAD + rows, PAD)] = rim
+        return carry
+
+    lax.fori_loop(0, count, rims, 0)
+    pl.semaphore_wait(barrier, members - 1 + 2 * NEAR)
+
+    away = line + 2 * half - 1
+    first = half * (depth - HALO)
+
+    def start_copy(j):
+        if j == 0:
+            src, dst, who = times_ref.at[1 - half], swap_in, at(line, 1 - half)
+        elif j == 1:
+            src, dst, who = speed_ref, swap_speed, at(line, 1 - half)
+        elif j < 4:
+            src = times_ref.at[j - 2, pl.ds(first, HALO)]
+            dst, who = halo_in.at[0, 1 - half], at(away, j - 2)
+        else:
+            src = speed_ref.at[pl.ds(first, HALO)]
+            dst, who = halo_speed.at[1 - half], at(away, j - 4)
+        slot = j if j < 2 else (2 if j < 4 else 4) + (1 - half)
+        return pltpu.make_async_remote_copy(
+            src_ref=src,
+            dst_ref=dst,
+            send_sem=start_send.at[j],
+            recv_sem=start_recv.at[slot],
+            device_id=who,
+            device_id_type=mesh_id,
+        )
+
+    def start_arrival(slot):
+        if slot == 0:
+            src, dst = times_ref.at[1 - half], swap_in
+        elif slot == 1:
+            src, dst = speed_ref, swap_speed
+        elif slot < 4:
+            src, dst = times_ref.at[0, pl.ds(0, HALO)], halo_in.at[0, slot - 2]
+        else:
+            src, dst = speed_ref.at[pl.ds(0, HALO)], halo_speed.at[slot - 4]
+        return pltpu.make_async_remote_copy(
+            src_ref=src,
+            dst_ref=dst,
+            send_sem=start_send.at[slot],
+            recv_sem=start_recv.at[slot],
+            device_id=at(line, 1 - half),
+            device_id_type=mesh_id,
+        )
+
+    for j in (2, 3, 0, 4, 5, 1):
+        start_copy(j).start()
+
+    at_lower = line == 0
+    at_upper = line == lines - 1
+
+    for i in range(depth):
+        tab[0, HALO + half * depth + i, inside] = times_ref[half, i]
+        spd[HALO + half * depth + i] = speed_ref[i]
+    for slot in range(6):
+        start_arrival(slot).wait_recv()
+    for i in range(depth):
+        tab[0, HALO + (1 - half) * depth + i, inside] = swap_in[i]
+        spd[HALO + (1 - half) * depth + i] = swap_speed[i]
+    for i in range(HALO):
+        spd[i] = halo_speed[0, i]
+        spd[HALO + own + i] = halo_speed[1, i]
+
+    def place_halo(exchange, side):
+        for i in range(HALO):
+            tab[side, i, inside] = jnp.where(at_lower, BIG, halo_in[exchange, 0, i])
+            tab[side, HALO + own + i, inside] = jnp.where(at_upper, BIG, halo_in[exchange, 1, i])
+
+    place_halo(0, 0)
+
+    lane = lax.broadcasted_iota(jnp.int32, (rows, lanes), 1)
+
+    def plane_value(side, plane):
+        centre = tab[side, plane, inside]
+        along_x = jnp.minimum(tab[side, plane - 1, inside], tab[side, plane + 1, inside])
+        along_y = jnp.minimum(
+            tab[side, plane, pl.ds(PAD - 1, rows)], tab[side, plane, pl.ds(PAD + 1, rows)]
+        )
+        before = jnp.where(lane == 0, BIG, pltpu.roll(centre, 1, 1))
+        after = jnp.where(lane == lanes - 1, BIG, pltpu.roll(centre, lanes - 1, 1))
+        along_z = jnp.minimum(before, after)
+        value = jnp.minimum(centre, godunov(along_x, along_y, along_z, spd[plane]))
+        outside = (at_lower & (plane < HALO)) | (at_upper & (plane >= HALO + own))
+        return jnp.maximum(value, jnp.where(outside, BIG, -BIG))
+
+    def sweep(side, total, plane_at, store):
+        def one(j, carry):
+            plane = plane_at(j)
+            store(plane, plane_value(side, plane))
+            return carry
+
+        lax.fori_loop(0, total, one, 0)
+
+    def into(side):
+        def store(plane, value):
+            tab[side, plane, inside] = value
+
+        return store
+
+    def into_stage(plane, value):
+        place = plane - HALO
+        for j in range(stas):
+            stage[(place // depth) * stas + j, place % depth] = value[piece * j : piece * (j + 1)]
+
+    def into_edge(side, exchange, lower):
+        def store(plane, value):
+            tab[side, plane, inside] = value
+            edge_out[exchange, 0 if lower else 1, plane - (HALO if lower else own)] = value
+
+        return store
+
+    def halo_copy(exchange, lower):
+        slot = 1 if lower else 0
+        return pltpu.make_async_remote_copy(
+            src_ref=edge_out.at[exchange - 1, 0 if lower else 1],
+            dst_ref=halo_in.at[exchange, slot],
+            send_sem=halo_send.at[exchange - 1, slot],
+            recv_sem=halo_recv.at[exchange - 1, slot],
+            device_id=at(line - 1 if lower else line + 1, half),
+            device_id_type=mesh_id,
+        )
+
+    def last_round(side, exchange):
+        sweep(side, HALO, lambda j: HALO + j, into_edge(1 - side, exchange - 1, True))
+        halo_copy(exchange, True).start()
+        sweep(side, HALO, lambda j: own + j, into_edge(1 - side, exchange - 1, False))
+        halo_copy(exchange, False).start()
+        sweep(side, own - 2 * HALO, lambda j: 2 * HALO + j, into(1 - side))
+
+    exchanges = ROUNDS // HALO
+    side = 0
+    for exchange in range(exchanges):
+        final = exchange == exchanges - 1
+        if exchange == 0:
+            for r in range(HALO - 1):
+                sweep(side, count - 2 - 2 * r, lambda j, r=r: r + 1 + j, into(1 - side))
+                side = 1 - side
+        else:
+            start = side
+            for r in range(HALO - 1):
+                sweep(side, own - 2 - 2 * r, lambda j, r=r: HALO + 1 + r + j, into(1 - side))
+                side = 1 - side
+            for lower in (True, False):
+                halo_copy(exchange, lower).wait()
+            side = start
+            place_halo(exchange, side)
+            for r in range(HALO - 1):
+                sweep(
+                    side,
+                    2 * HALO,
+                    lambda j, r=r: jnp.where(j < HALO, r + 1 + j, own - 1 - r + j),
+                    into(1 - side),
+                )
+                side = 1 - side
+        if final:
+            sweep(side, own, lambda j: HALO + j, into_stage)
+        else:
+            last_round(side, exchange + 1)
+            side = 1 - side
+
+    def block_copy(j):
+        other = (member + j) % members
+        return pltpu.make_async_remote_copy(
+            src_ref=stage.at[other],
+            dst_ref=arrived.at[station],
+            send_sem=all_send.at[j],
+            recv_sem=all_recv.at[station],
+            device_id=member_at(other),
+            device_id_type=mesh_id,
+        )
+
+    def block_arrival(j):
+        other = (member + j) % members
+        source = NEAR * (other % stas) + other // stas
+        return pltpu.make_async_remote_copy(
+            src_ref=stage.at[other],
+            dst_ref=arrived.at[source],
+            send_sem=all_send.at[j],
+            recv_sem=all_recv.at[source],
+            device_id=member_at(other),
+            device_id_type=mesh_id,
+        )
+
+    def start_block(j, carry):
+        block_copy(j).start()
+        return carry
+
+    def end_block(j, carry):
+        block_copy(j).wait_send()
+        block_arrival(j).wait_recv()
+        return carry
+
+    lax.fori_loop(1, members, start_block, 0)
+    arrived[station] = stage[member]
+    for j in range(6):
+        start_copy(j).wait_send()
+    lax.fori_loop(1, members, end_block, 0)
+    refined_ref[...] = arrived[...]
+
+
+def refined_tables(coarse_times, speed):
+    per_device, depth, rows, lanes = coarse_times.shape
+    stas = lax.axis_size("sta")
+    stations = per_device * stas
+    assert per_device == NEAR and ROUNDS % HALO == 0 and HALO <= depth
+    piece = rows // stas
+    own = NEAR * depth
+    count = own + 2 * HALO
+    exchanges = ROUNDS // HALO
+    plane = (rows, lanes)
+    vmem = pl.BlockSpec(memory_space=pltpu.VMEM)
+    dma = pltpu.SemaphoreType.DMA
+    return pl.pallas_call(
+        travel_kernel,
+        out_shape=jax.ShapeDtypeStruct((stations, depth, piece, lanes), jnp.float32),
+        in_specs=[vmem, vmem],
+        out_specs=vmem,
+        scratch_shapes=[
+            pltpu.VMEM((2, count, rows + 2 * PAD, lanes), jnp.float32),
+            pltpu.VMEM((count,) + plane, jnp.float32),
+            pltpu.VMEM((depth,) + plane, jnp.float32),
+            pltpu.VMEM((depth,) + plane, jnp.float32),
+            pltpu.VMEM((exchanges, 2, HALO) + plane, jnp.float32),
+            pltpu.VMEM((2, HALO) + plane, jnp.float32),
+            pltpu.VMEM((exchanges - 1, 2, HALO) + plane, jnp.float32),
+            pltpu.VMEM((NEAR * stas, depth, piece, lanes), jnp.float32),
+            pltpu.VMEM((stations, depth, piece, lanes), jnp.float32),
+            dma((6,)),
+            dma((6,)),
+            dma((exchanges - 1, 2)),
+            dma((exchanges - 1, 2)),
+            dma((NEAR * stas,)),
+            dma((stations,)),
+        ],
+        compiler_params=pltpu.CompilerParams(collective_id=1, has_side_effects=True),
+        name="travel",
+    )(coarse_times, speed)
 
 
 def misfit_block(event_pair, flat_tables):
@@ -169,22 +467,7 @@
 
 
 def body(coarse_times, model_map, slowness, picks, pick_mask):
-    levels = lax.broadcasted_iota(jnp.int32, (slowness.shape[0], 1, 1, 1), 0)
-    speed = grid_step * jnp.sum(
-        jnp.where(model_map[None] == levels, slowness[:, None, None, None], 0.0), 0
-    )
-    position_space = lax.axis_index("space")
-    devices_space = lax.axis_size("space")
-    at_lower = position_space == 0
-    at_upper = position_space == devices_space - 1
-    tables = coarse_times
-
-    def one_round(round_index, tables):
-        extended = extended_2(tables, (("space", 1),), 1)
-        return relax(close_rims(extended, 1, at_lower, at_upper), speed)
-
-    tables = lax.fori_loop(0, ROUNDS, one_round, tables)
-    refined = lax.all_to_all(tables, "sta", split_axis=2, concat_axis=0, tiled=True)
+    refined = refined_tables(coarse_times, speed_of(model_map, slowness))
     stations = refined.shape[0]
     flat_tables = refined.reshape(stations, -1)
     observed = pick_mask.astype(jnp.float32)

time: 231 us -> 114 us (0.49)
  starting transfers between devices: 99.1 us -> 0 us
  waiting for transfers between devices: 20.1 us -> 0 us
  Pallas kernels: 64.5 us -> 72.1 us
  other arithmetic: 36.5 us -> 32.7 us
    ppermute x24 -> x0, starting transfers between devices: 78.4 us -> none  [the longest x12 62.9 us: extended_2(): lax.ppermute(lax.slice_in_dim(block, block.shape[dim] - width, None, axis...]
    pallas_call x0 -> x2, Pallas kernels: none -> 54.5 us  [the longest x1 52.8 us: refined_tables(): pl.pallas_call(travel_kernel, out_shape=jax.ShapeDtypeStruct((stations, d...]
    pallas_call x1, Pallas kernels: 64.5 us -> 17.7 us  [global_stats(): pl.pallas_call(stats_kernel, out_shape=jax.ShapeDtypeStruct(local.shape,...]
    all_to_all x1 -> x0, starting transfers between devices: 20.7 us -> none  [body(): lax.all_to_all(tables, 'sta', split_axis=2, concat_axis=0, tiled=True)]
    ppermute x24 -> x0, waiting for transfers between devices: 11.5 us -> none  [the longest x12 11.5 us: extended_2(): lax.ppermute(lax.slice_in_dim(block, block.shape[dim] - width, None, axis...]
    all_to_all x1 -> x0, waiting for transfers between devices: 8.57 us -> none  [body(): lax.all_to_all(tables, 'sta', split_axis=2, concat_axis=0, tiled=True)]
    min x12 -> x0, other arithmetic: 4 us -> none  [relax(): return jnp.minimum(centre, godunov(along_x, along_y, along_z, speed[None]))]
  transfers between devices with their start and end apart: 25 -> 0, of which waited for: 13 -> 0; matrix products, arithmetic and copies ran while one was open for 0% -> 0% of each run, Pallas kernels for 0% -> 0%
where the time goes in v2:
time: 114 us
  Pallas kernels  72.1 us (63%)
  other arithmetic  32.7 us (29%)
  local copies, waits for them, and re-layouts  8.03 us (7%)
    pallas_call x1, Pallas kernels, refined_tables(): pl.pallas_call(travel_kernel, out_shape=jax.ShapeDtypeStruct((stations, d...  52.8 us
    pallas_call x1, Pallas kernels, global_stats(): pl.pallas_call(stats_kernel, out_shape=jax.ShapeDtypeStruct(local.shape,...  17.7 us
    reduce_sum x8, other arithmetic, misfit_block(): return jnp.sum(observed[:, :, None] * deviation * deviation, 1)  14 us
    reduce_sum x8, other arithmetic, misfit_block(): jnp.sum(observed[:, :, None] * residual, 1) / pick_count[:, None]  9.54 us
    mul x1, other arithmetic, body(): density = cell_weights * scale[:, None]  3.58 us
    reduce_sum x1, other arithmetic, body(): top_score, mass_sum = global_stats(local_top, jnp.sum(cell_weights, 1))  2.3 us

profile of v2, /device:TPU:1, one launch (start us, length us, event | category | flops | bytes accessed | tf_op | source)
XLA Modules:
  0.0 114.0 jit_solution(7833046852319817866)
XLA Ops:
  0.6 1.2 %pad_bitcast_fusion.table_ref = f32[1,128]{1,0:T(1,128)} fusion(f32[64]{0:T(128)} %param.9), kind=kLoop, calls=%fused_computation.16 | loop fusion | bytes 768 | tf_op jit(solution)/shard_map/reshape | solution.py:126
  1.8 1.7 %speed.1.speed_ref = f32[5,32,128]{2,1,0:T(8,128)} custom-call(f32[1,128]{1,0:T(1,128)} %pad_bitcast_fusion.table_ref, s32[5,32,128]{2,1,0:T(8,128)} %map_ref.1), custom_call_target="tpu_custom_call" | custom-call | tf_op jit(solution)/shard_map/speed/pallas_call | solution.py:127
  3.5 52.8 %travel.1 = f32[16,5,4,128]{3,2,1,0:T(4,128)S(1)} custom-call(f32[2,5,32,128]{3,2,1,0:T(8,128)} %times_ref.1, f32[5,32,128]{2,1,0:T(8,128)} %speed.1.speed_ref), custom_call_target="tpu_custom_call" | custom-call | tf_op jit(solution)/shard_map/travel/pallas_call | solution.py:433
  56.4 0.7 convert_element_type.5
  57.2 0.8 reshape.88
  58.0 26.5 %while.11 = (s32[]{:T(128)}, f32[8,32,2560]{2,1,0:T(8,128)S(1)}, f32[8,32,16]{1,0,2:T(8,128)S(1)}, f32[8,32,16]{1,0,2:T(8,128)S(1)}, f32[16,5,4,128]{3,2,1,0:T(4...) while((s32[]{:T(128)}, f32[8,32,2560]{2,1,0:T(8,128)S(1)}, f32[8,32,16]{1,0,2:T(8,128)S(1)}, ...), condition=%wide.wide.region_4.5_spmd, body=%wide.wide.region_0.4_spmd.sunk | while | flops 10404322 | bytes 2648417 | solution.py:474
  58.2 1.2 %fusion.8 = f32[32,2560]{1,0:T(8,128)S(1)} fusion(f32[16,2560]{1,0:T(8,128)S(1)} %get-tuple-element.138, f32[32,16]{1,0:T(8,128)S(1)} %copy.21, f32[32,16]{1,0:T(8,128)S(1)} %copy.22), kind=kLoop, calls=%fused_computation.3.clone.clone.1 | loop fusion | flops 3850240 | bytes 495616 | tf_op jit(solution)/shard_map/while/body/eval_jaxpr/reduce_sum | solution.py:464
  59.4 0.1 broadcast_divide_fusion.3
  59.5 1.8 %fusion.9 = f32[32,2560]{1,0:T(8,128)S(1)} fusion(f32[32,2560]{1,0:T(8,128)S(1)} %broadcast_divide_fusion.3, f32[16,2560]{1,0:T(8,128)S(1)} %get-tuple-element.138, f32[32,16]{1,0:T(8,128)S(1)} %copy.21, f32[32,16]{1,0:T(8,128)S(1)} %copy.22), kind=kLoop, calls=%fused_computation.4.clone.clone.1 | loop fusion | flops 6471680 | bytes 823296 | tf_op jit(solution)/shard_map/while/body/eval_jaxpr/reduce_sum | solution.py:466
  61.5 1.2 %fusion.8 = f32[32,2560]{1,0:T(8,128)S(1)} fusion(f32[16,2560]{1,0:T(8,128)S(1)} %get-tuple-element.138, f32[32,16]{1,0:T(8,128)S(1)} %copy.21, f32[32,16]{1,0:T(8,128)S(1)} %copy.22), kind=kLoop, calls=%fused_computation.3.clone.clone.1 | loop fusion | flops 3850240 | bytes 495616 | tf_op jit(solution)/shard_map/while/body/eval_jaxpr/reduce_sum | solution.py:464
  62.8 1.8 %fusion.9 = f32[32,2560]{1,0:T(8,128)S(1)} fusion(f32[32,2560]{1,0:T(8,128)S(1)} %broadcast_divide_fusion.3, f32[16,2560]{1,0:T(8,128)S(1)} %get-tuple-element.138, f32[32,16]{1,0:T(8,128)S(1)} %copy.21, f32[32,16]{1,0:T(8,128)S(1)} %copy.22), kind=kLoop, calls=%fused_computation.4.clone.clone.1 | loop fusion | flops 6471680 | bytes 823296 | tf_op jit(solution)/shard_map/while/body/eval_jaxpr/reduce_sum | solution.py:466
  64.8 1.2 %fusion.8 = f32[32,2560]{1,0:T(8,128)S(1)} fusion(f32[16,2560]{1,0:T(8,128)S(1)} %get-tuple-element.138, f32[32,16]{1,0:T(8,128)S(1)} %copy.21, f32[32,16]{1,0:T(8,128)S(1)} %copy.22), kind=kLoop, calls=%fused_computation.3.clone.clone.1 | loop fusion | flops 3850240 | bytes 495616 | tf_op jit(solution)/shard_map/while/body/eval_jaxpr/reduce_sum | solution.py:464
  66.1 1.8 %fusion.9 = f32[32,2560]{1,0:T(8,128)S(1)} fusion(f32[32,2560]{1,0:T(8,128)S(1)} %broadcast_divide_fusion.3, f32[16,2560]{1,0:T(8,128)S(1)} %get-tuple-element.138, f32[32,16]{1,0:T(8,128)S(1)} %copy.21, f32[32,16]{1,0:T(8,128)S(1)} %copy.22), kind=kLoop, calls=%fused_computation.4.clone.clone.1 | loop fusion | flops 6471680 | bytes 823296 | tf_op jit(solution)/shard_map/while/body/eval_jaxpr/reduce_sum | solution.py:466
  68.1 1.2 %fusion.8 = f32[32,2560]{1,0:T(8,128)S(1)} fusion(f32[16,2560]{1,0:T(8,128)S(1)} %get-tuple-element.138, f32[32,16]{1,0:T(8,128)S(1)} %copy.21, f32[32,16]{1,0:T(8,128)S(1)} %copy.22), kind=kLoop, calls=%fused_computation.3.clone.clone.1 | loop fusion | flops 3850240 | bytes 495616 | tf_op jit(solution)/shard_map/while/body/eval_jaxpr/reduce_sum | solution.py:464
  69.4 1.8 %fusion.9 = f32[32,2560]{1,0:T(8,128)S(1)} fusion(f32[32,2560]{1,0:T(8,128)S(1)} %broadcast_divide_fusion.3, f32[16,2560]{1,0:T(8,128)S(1)} %get-tuple-element.138, f32[32,16]{1,0:T(8,128)S(1)} %copy.21, f32[32,16]{1,0:T(8,128)S(1)} %copy.22), kind=kLoop, calls=%fused_computation.4.clone.clone.1 | loop fusion | flops 6471680 | bytes 823296 | tf_op jit(solution)/shard_map/while/body/eval_jaxpr/reduce_sum | solution.py:466
  71.4 1.2 %fusion.8 = f32[32,2560]{1,0:T(8,128)S(1)} fusion(f32[16,2560]{1,0:T(8,128)S(1)} %get-tuple-element.138, f32[32,16]{1,0:T(8,128)S(1)} %copy.21, f32[32,16]{1,0:T(8,128)S(1)} %copy.22), kind=kLoop, calls=%fused_computation.3.clone.clone.1 | loop fusion | flops 3850240 | bytes 495616 | tf_op jit(solution)/shard_map/while/body/eval_jaxpr/reduce_sum | solution.py:464
  72.7 1.8 %fusion.9 = f32[32,2560]{1,0:T(8,128)S(1)} fusion(f32[32,2560]{1,0:T(8,128)S(1)} %broadcast_divide_fusion.3, f32[16,2560]{1,0:T(8,128)S(1)} %get-tuple-element.138, f32[32,16]{1,0:T(8,128)S(1)} %copy.21, f32[32,16]{1,0:T(8,128)S(1)} %copy.22), kind=kLoop, calls=%fused_computation.4.clone.clone.1 | loop fusion | flops 6471680 | bytes 823296 | tf_op jit(solution)/shard_map/while/body/eval_jaxpr/reduce_sum | solution.py:466
  74.7 1.2 %fusion.8 = f32[32,2560]{1,0:T(8,128)S(1)} fusion(f32[16,2560]{1,0:T(8,128)S(1)} %get-tuple-element.138, f32[32,16]{1,0:T(8,128)S(1)} %copy.21, f32[32,16]{1,0:T(8,128)S(1)} %copy.22), kind=kLoop, calls=%fused_computation.3.clone.clone.1 | loop fusion | flops 3850240 | bytes 495616 | tf_op jit(solution)/shard_map/while/body/eval_jaxpr/reduce_sum | solution.py:464
  76.1 1.8 %fusion.9 = f32[32,2560]{1,0:T(8,128)S(1)} fusion(f32[32,2560]{1,0:T(8,128)S(1)} %broadcast_divide_fusion.3, f32[16,2560]{1,0:T(8,128)S(1)} %get-tuple-element.138, f32[32,16]{1,0:T(8,128)S(1)} %copy.21, f32[32,16]{1,0:T(8,128)S(1)} %copy.22), kind=kLoop, calls=%fused_computation.4.clone.clone.1 | loop fusion | flops 6471680 | bytes 823296 | tf_op jit(solution)/shard_map/while/body/eval_jaxpr/reduce_sum | solution.py:466
  78.0 1.2 %fusion.8 = f32[32,2560]{1,0:T(8,128)S(1)} fusion(f32[16,2560]{1,0:T(8,128)S(1)} %get-tuple-element.138, f32[32,16]{1,0:T(8,128)S(1)} %copy.21, f32[32,16]{1,0:T(8,128)S(1)} %copy.22), kind=kLoop, calls=%fused_computation.3.clone.clone.1 | loop fusion | flops 3850240 | bytes 495616 | tf_op jit(solution)/shard_map/while/body/eval_jaxpr/reduce_sum | solution.py:464
  79.4 1.8 %fusion.9 = f32[32,2560]{1,0:T(8,128)S(1)} fusion(f32[32,2560]{1,0:T(8,128)S(1)} %broadcast_divide_fusion.3, f32[16,2560]{1,0:T(8,128)S(1)} %get-tuple-element.138, f32[32,16]{1,0:T(8,128)S(1)} %copy.21, f32[32,16]{1,0:T(8,128)S(1)} %copy.22), kind=kLoop, calls=%fused_computation.4.clone.clone.1 | loop fusion | flops 6471680 | bytes 823296 | tf_op jit(solution)/shard_map/while/body/eval_jaxpr/reduce_sum | solution.py:466
  81.4 1.2 %fusion.8 = f32[32,2560]{1,0:T(8,128)S(1)} fusion(f32[16,2560]{1,0:T(8,128)S(1)} %get-tuple-element.138, f32[32,16]{1,0:T(8,128)S(1)} %copy.21, f32[32,16]{1,0:T(8,128)S(1)} %copy.22), kind=kLoop, calls=%fused_computation.3.clone.clone.1 | loop fusion | flops 3850240 | bytes 495616 | tf_op jit(solution)/shard_map/while/body/eval_jaxpr/reduce_sum | solution.py:464
  82.7 1.8 %fusion.9 = f32[32,2560]{1,0:T(8,128)S(1)} fusion(f32[32,2560]{1,0:T(8,128)S(1)} %broadcast_divide_fusion.3, f32[16,2560]{1,0:T(8,128)S(1)} %get-tuple-element.138, f32[32,16]{1,0:T(8,128)S(1)} %copy.21, f32[32,16]{1,0:T(8,128)S(1)} %copy.22), kind=kLoop, calls=%fused_computation.4.clone.clone.1 | loop fusion | flops 6471680 | bytes 823296 | tf_op jit(solution)/shard_map/while/body/eval_jaxpr/reduce_sum | solution.py:466
  84.5 1.5 %copy-done = f32[8,32,2560]{2,1,0:T(8,128)} copy-done((f32[8,32,2560]{2,1,0:T(8,128)}, f32[8,32,2560]{2,1,0:T(8,128)S(1)}, u32[]{:S(2)}) %copy-start) | copy-done | bytes 2621464
  86.0 0.3 fusion.3
  86.2 2.3 %exponential_reduce_fusion = (f32[8,32]{1,0:T(8,128)S(1)}, f32[8,32,2560]{2,1,0:T(8,128)S(1)}) fusion(f32[8,32]{1,0:T(8,128)S(1)} %fusion.3, f32[8,32,2560]{2,1,0:T(8,128)} %copy-done), kind=kLoop, calls=%fused_computation.9 | loop fusion | flops 1965824 | bytes 5244928 | tf_op jit(solution)/shard_map/reduce_sum | solution.py:481
  88.7 0.6 pad_maximum_fusion.local_ref
  89.3 17.7 %stats.1 = f32[4,128]{1,0:T(4,128)} custom-call(f32[4,128]{1,0:T(4,128)} %pad_maximum_fusion.local_ref), custom_call_target="tpu_custom_call" | custom-call | tf_op jit(solution)/shard_map/stats/pallas_call | solution.py:95
  107.0 0.8 bitcast_divide_fusion
  107.8 2.0 %div.29 = f32[256,5,4,128]{3,2,1,0:T(4,128)} reshape(f32[8,32,2560]{2,1,0:T(8,128)S(1)} %get-tuple-element.53) | data formatting | bytes 5242880 | tf_op jit(solution)/shard_map/div | solution.py:478
  109.8 3.6 %exponential_multiply_fusion = f32[256,5,4,128]{3,2,1,0:T(4,128)} fusion(f32[256,5,4,128]{3,2,1,0:T(4,128)} %div.29, f32[256]{0:T(256)S(1)} %bitcast_divide_fusion, f32[256]{0:T(256)S(1)} %sub.48), kind=kLoop, calls=%fused_computation.10 | loop fusion | flops 1310720 | bytes 5244928 | tf_op jit(solution)/shard_map/mul | solution.py:483
  113.4 0.7 copy.33
  (58 shorter events, 2.8 us)
Async XLA Ops:
  56.3 1.7 %copy-start.1 = (f32[16,5,4,128]{3,2,1,0:T(4,128)}, f32[16,5,4,128]{3,2,1,0:T(4,128)S(1)}, u32[]{:S(2)}) copy-start(f32[16,5,4,128]{3,2,1,0:T(4,128)S(1)} %travel.1) | copy-start | bytes 491524
  84.5 1.5 %copy-start = (f32[8,32,2560]{2,1,0:T(8,128)}, f32[8,32,2560]{2,1,0:T(8,128)S(1)}, u32[]{:S(2)}) copy-start(f32[8,32,2560]{2,1,0:T(8,128)S(1)} %get-tuple-element.29) | copy-start | bytes 7864324
  109.8 3.6 %copy-start.2 = (f32[16,5,4,128]{3,2,1,0:T(4,128)S(1)}, f32[16,5,4,128]{3,2,1,0:T(4,128)}, u32[]{:S(2)}) copy-start(f32[16,5,4,128]{3,2,1,0:T(4,128)} %get-tuple-element.145) | copy-start | bytes 491524

commit v3 on v2

--- a/solution.py
+++ b/solution.py
@@ -10,104 +10,7 @@
 BIG = 1000000.0
 pick_sigma = 0.25
 grid_step = 1.0
-block_events = 32
 NEAR = 2
-
-
-def merge_softmax_stats(top, mass, slots, count):
-    best = top
-    for k in range(count):
-        best = jnp.maximum(best, slots[k, 0:2])
-    total = mass * jnp.exp(top - best)
-    for k in range(count):
-        total = total + slots[k, 2:4] * jnp.exp(slots[k, 0:2] - best)
-    return best, total
-
-
-def stats_kernel(local_ref, out_ref, first, second, mid, send_sem, recv_sem):
-    space = lax.axis_index("space")
-    sta = lax.axis_index("sta")
-    stas = lax.axis_size("sta")
-    lines = lax.axis_size("space") // NEAR
-    line = space // NEAR
-    member = (space % NEAR) * stas + sta
-    members = NEAR * stas
-
-    def member_id(k):
-        other = (member + k) % members
-        return {"space": line * NEAR + other // stas, "sta": other % stas}
-
-    def line_id(k):
-        other = (line + k) % lines
-        return {"space": other * NEAR + space % NEAR, "sta": sta}
-
-    barrier = pltpu.get_barrier_semaphore()
-
-    def greet(ids, count):
-        def one(k, carry):
-            pl.semaphore_signal(barrier, inc=1, device_id=ids(k), device_id_type=pl.DeviceIdType.MESH)
-            return carry
-
-        lax.fori_loop(1, count, one, 0)
-
-    greet(member_id, members)
-    greet(line_id, lines)
-    pl.semaphore_wait(barrier, members + lines - 2)
-
-    def exchange(src, slots, ids, count, phase):
-        def copy(k):
-            return pltpu.make_async_remote_copy(
-                src_ref=src,
-                dst_ref=slots.at[k - 1],
-                send_sem=send_sem.at[phase, k - 1],
-                recv_sem=recv_sem.at[phase, k - 1],
-                device_id=ids(k),
-                device_id_type=pl.DeviceIdType.MESH,
-            )
-
-        def start(k, carry):
-            copy(k).start()
-            return carry
-
-        def wait(k, carry):
-            copy(k).wait()
-            return carry
-
-        lax.fori_loop(1, count, start, 0)
-        lax.fori_loop(1, count, wait, 0)
-
-    exchange(local_ref, first, member_id, members, 0)
-    top, mass = merge_softmax_stats(local_ref[0:2], local_ref[2:4], first, members - 1)
-    mid[0:2] = top
-    mid[2:4] = mass
-    exchange(mid, second, line_id, lines, 1)
-    top, mass = merge_softmax_stats(top, mass, second, lines - 1)
-    out_ref[0:2] = top
-    out_ref[2:4] = mass
-
-
-def global_stats(top, mass):
-    events = top.shape[0]
-    local = jnp.concatenate([top.reshape(2, -1), mass.reshape(2, -1)], 0)
-    members = NEAR * lax.axis_size("sta")
-    lines = lax.axis_size("space") // NEAR
-    longest = max(members, lines)
-    out = pl.pallas_call(
-        stats_kernel,
-        out_shape=jax.ShapeDtypeStruct(local.shape, jnp.float32),
-        in_specs=[pl.BlockSpec(memory_space=pltpu.VMEM)],
-        out_specs=pl.BlockSpec(memory_space=pltpu.VMEM),
-        scratch_shapes=[
-            pltpu.VMEM((members - 1,) + local.shape, jnp.float32),
-            pltpu.VMEM((lines - 1,) + local.shape, jnp.float32),
-            pltpu.VMEM(local.shape, jnp.float32),
-            pltpu.SemaphoreType.DMA((2, longest)),
-            pltpu.SemaphoreType.DMA((2, longest)),
-        ],
-        compiler_params=pltpu.CompilerParams(collective_id=0, has_side_effects=True),
-        name="stats",
-    )(local)
-    return out[0:2].reshape(events), out[2:4].reshape(events)
 
 
 HALO = 4
@@ -457,32 +360,266 @@
     )(coarse_times, speed)
 
 
-def misfit_block(event_pair, flat_tables):
-    arrivals, observed = event_pair
-    pick_count = jnp.sum(observed, 1)
-    residual = arrivals[:, :, None] - flat_tables[None]
-    anchor_shift = jnp.sum(observed[:, :, None] * residual, 1) / pick_count[:, None]
-    deviation = residual - anchor_shift[:, None, :]
-    return jnp.sum(observed[:, :, None] * deviation * deviation, 1)
+EVENT_TILE = 8
+
+
+def locate_kernel(
+    times_ref,
+    picks_ref,
+    mask_ref,
+    weight_ref,
+    peak_ref,
+    stats_ref,
+    pick_rows,
+    mask_rows,
+    picked_sum,
+    score,
+    lane_mass,
+    first,
+    second,
+    local,
+    mid,
+    send_sem,
+    recv_sem,
+):
+    space = lax.axis_index("space")
+    sta = lax.axis_index("sta")
+    stas = lax.axis_size("sta")
+    lines = lax.axis_size("space") // NEAR
+    line = space // NEAR
+    member = (space % NEAR) * stas + sta
+    members = NEAR * stas
+
+    def member_id(k):
+        other = (member + k) % members
+        return {"space": line * NEAR + other // stas, "sta": other % stas}
+
+    def line_id(k):
+        return {"space": ((line + k) % lines) * NEAR + space % NEAR, "sta": sta}
+
+    barrier = pltpu.get_barrier_semaphore()
+
+    def greet(ids, count):
+        def one(k, carry):
+            pl.semaphore_signal(barrier, inc=1, device_id=ids(k), device_id_type=pl.DeviceIdType.MESH)
+            return carry
+
+        lax.fori_loop(1, count, one, 0)
+
+    greet(member_id, members)
+    greet(line_id, lines)
+
+    stations, events = picks_ref.shape
+    rows, _, lanes = weight_ref.shape
+    blocks = events // lanes
+
+    for b in range(blocks):
+        cut = pl.ds(b * lanes, lanes)
+        part = picks_ref[:, cut]
+        blank = jnp.zeros((lanes - stations, lanes), jnp.float32)
+        pick_rows[cut] = jnp.concatenate([part, blank], 0).T
+        part = mask_ref[:, cut].astype(jnp.float32)
+        blank = jnp.zeros((lanes - 3 * stations, lanes), jnp.float32)
+        mask_rows[cut] = jnp.concatenate([part, part, part, blank], 0).T
+
+    chosen = mask_rows[...].astype(jnp.bfloat16)
+    blank = jnp.zeros((lanes - 3 * stations, lanes), jnp.float32)
+
+    def pieces(row):
+        part = times_ref[pl.ds(row, stations, stride=rows)]
+        high = part.astype(jnp.bfloat16).astype(jnp.float32)
+        rest = part - high
+        middle = rest.astype(jnp.bfloat16).astype(jnp.float32)
+        return jnp.concatenate([high, middle, rest - middle, blank], 0).astype(jnp.bfloat16)
+
+    def sums(pair, carry):
+        right = jnp.concatenate([pieces(2 * pair), pieces(2 * pair + 1)], 1)
+        both = jnp.dot(chosen, right, preferred_element_type=jnp.float32)
+        picked_sum[2 * pair] = both[:, :lanes]
+        picked_sum[2 * pair + 1] = both[:, lanes:]
+        return carry
+
+    lax.fori_loop(0, rows // 2, sums, 0)
+
+    def tile(index, carry):
+        cut = pl.ds(pl.multiple_of(index * EVENT_TILE, EVENT_TILE), EVENT_TILE)
+        shape = (EVENT_TILE, lanes)
+        pick = pick_rows[cut]
+        mask = mask_rows[cut]
+        arrival = [jnp.broadcast_to(pick[:, s : s + 1], shape) for s in range(stations)]
+        seen = [jnp.broadcast_to(mask[:, s : s + 1], shape) for s in range(stations)]
+        number = seen[0]
+        total = seen[0] * arrival[0]
+        for s in range(1, stations):
+            number = number + seen[s]
+            total = total + seen[s] * arrival[s]
+
+        def row(r, top):
+            shift = (total - picked_sum[r, cut]) / number
+            misfit = None
+            for s in range(stations):
+                time = jnp.broadcast_to(times_ref[pl.ds(s * rows + r, 1)], shape)
+                deviation = (arrival[s] - time) - shift
+                term = seen[s] * (deviation * deviation)
+                misfit = term if misfit is None else misfit + term
+            value = (-0.5 / (pick_sigma * pick_sigma)) * misfit
+            score[r] = value
+            return jnp.maximum(top, value)
+
+        top = lax.fori_loop(0, rows, row, jnp.full(shape, -3.0e38, jnp.float32))
+
+        def weigh(r, mass):
+            weight = jnp.exp(score[r] - top)
+            weight_ref[r, cut] = weight
+            return mass + weight
+
+        mass = lax.fori_loop(0, rows, weigh, jnp.zeros(shape, jnp.float32))
+        peak_ref[cut] = top
+        lane_mass[cut] = mass
+        return carry
+
+    lax.fori_loop(0, events // EVENT_TILE, tile, 0)
+
+    for b in range(blocks):
+        cut = pl.ds(b * lanes, lanes)
+        peak = peak_ref[cut].T
+        top = jnp.max(peak, 0, keepdims=True)
+        mass = jnp.sum(lane_mass[cut].T * jnp.exp(peak - top), 0, keepdims=True)
+        local[pl.ds(b, 1)] = top
+        local[pl.ds(blocks + b, 1)] = mass
+
+    pl.semaphore_wait(barrier, members + lines - 2)
+
+    def exchange(src, slots, ids, count, phase):
+        def copy(k):
+            return pltpu.make_async_remote_copy(
+                src_ref=src,
+                dst_ref=slots.at[k - 1],
+                send_sem=send_sem.at[phase, k - 1],
+                recv_sem=recv_sem.at[phase, k - 1],
+                device_id=ids(k),
+                device_id_type=pl.DeviceIdType.MESH,
+            )
+
+        def start(k, carry):
+            copy(k).start()
+            return carry
+
+        def wait(k, carry):
+            copy(k).wait()
+            return carry
+
+        lax.fori_loop(1, count, start, 0)
+        lax.fori_loop(1, count, wait, 0)
+
+    def merged(top, mass, slots, count):
+        best = top
+        for k in range(count):
+            best = jnp.maximum(best, slots[k, :blocks])
+        total = mass * jnp.exp(top - best)
+        for k in range(count):
+            total = total + slots[k, blocks:] * jnp.exp(slots[k, :blocks] - best)
+        return best, total
+
+    exchange(local, first, member_id, members, 0)
+    top, mass = merged(local[:blocks], local[blocks:], first, members - 1)
+    mid[:blocks] = top
+    mid[blocks:] = mass
+    exchange(mid, second, line_id, lines, 1)
+    top, mass = merged(top, mass, second, lines - 1)
+    stats_ref[:blocks] = top
+    stats_ref[blocks:] = mass
+
+
+def density_kernel(weight_ref, peak_ref, stats_ref, out_ref, scale, chunk, sem):
+    rows, events, lanes = weight_ref.shape
+    blocks = events // lanes
+    size = chunk.shape[1] // rows
+    for b in range(blocks):
+        cut = pl.ds(b * lanes, lanes)
+        top = jnp.broadcast_to(stats_ref[pl.ds(b, 1)], (lanes, lanes)).T
+        mass = jnp.broadcast_to(stats_ref[pl.ds(blocks + b, 1)], (lanes, lanes)).T
+        scale[cut] = jnp.exp(peak_ref[cut] - top) / mass
+
+    def copy(c, slot):
+        return pltpu.make_async_copy(
+            chunk.at[slot], out_ref.at[pl.ds(c * size * rows, size * rows)], sem.at[slot]
+        )
+
+    slots = chunk.shape[0]
+    chunks = events // size
+    for c in range(chunks):
+        slot = c % slots
+        if c >= slots:
+            copy(c - slots, slot).wait()
+        for t in range(size // EVENT_TILE):
+            cut = pl.ds(c * size + t * EVENT_TILE, EVENT_TILE)
+            factor = scale[cut]
+            for r in range(rows):
+                chunk[slot, pl.ds(t * EVENT_TILE * rows + r, EVENT_TILE, stride=rows)] = (
+                    weight_ref[r, cut] * factor
+                )
+        copy(c, slot).start()
+    for c in range(chunks - slots, chunks):
+        copy(c, c % slots).wait()
+
+
+def event_density(refined, picks, pick_mask):
+    stations, depth, piece, lanes = refined.shape
+    events = picks.shape[0]
+    rows = depth * piece
+    assert 3 * stations <= lanes and events % lanes == 0 and rows % 2 == 0
+    blocks = events // lanes
+    members = NEAR * lax.axis_size("sta")
+    lines = lax.axis_size("space") // NEAR
+    longest = max(members, lines)
+    vmem = pl.BlockSpec(memory_space=pltpu.VMEM)
+    wide = (events, lanes)
+    message = (2 * blocks, lanes)
+    f32 = jnp.float32
+    weight, peak, stats = pl.pallas_call(
+        locate_kernel,
+        out_shape=(
+            jax.ShapeDtypeStruct((rows,) + wide, f32),
+            jax.ShapeDtypeStruct(wide, f32),
+            jax.ShapeDtypeStruct(message, f32),
+        ),
+        in_specs=[vmem] * 3,
+        out_specs=[vmem] * 3,
+        scratch_shapes=[
+            pltpu.VMEM(wide, f32),
+            pltpu.VMEM(wide, f32),
+            pltpu.VMEM((rows,) + wide, f32),
+            pltpu.VMEM((rows, EVENT_TILE, lanes), f32),
+            pltpu.VMEM(wide, f32),
+            pltpu.VMEM((members - 1,) + message, f32),
+            pltpu.VMEM((lines - 1,) + message, f32),
+            pltpu.VMEM(message, f32),
+            pltpu.VMEM(message, f32),
+            pltpu.SemaphoreType.DMA((2, longest)),
+            pltpu.SemaphoreType.DMA((2, longest)),
+        ],
+        compiler_params=pltpu.CompilerParams(collective_id=0, has_side_effects=True),
+        name="locate",
+    )(refined.reshape(stations * rows, lanes), picks.T, pick_mask.T)
+    density = pl.pallas_call(
+        density_kernel,
+        out_shape=jax.ShapeDtypeStruct((events * rows, lanes), f32),
+        in_specs=[vmem] * 3,
+        out_specs=pl.BlockSpec(memory_space=pl.ANY),
+        scratch_shapes=[
+            pltpu.VMEM(wide, f32),
+            pltpu.VMEM((4, 32 * rows, lanes), f32),
+            pltpu.SemaphoreType.DMA((4,)),
+        ],
+        name="density",
+    )(weight, peak, stats)
+    return density.reshape(events, depth, piece, lanes)
 
 
 def body(coarse_times, model_map, slowness, picks, pick_mask):
     refined = refined_tables(coarse_times, speed_of(model_map, slowness))
-    stations = refined.shape[0]
-    flat_tables = refined.reshape(stations, -1)
-    observed = pick_mask.astype(jnp.float32)
-    blocks = lax.map(
-        lambda event_pair: misfit_block(event_pair, flat_tables),
-        (picks.reshape(-1, block_events, stations), observed.reshape(-1, block_events, stations)),
-    )
-    score = -0.5 * blocks.reshape(picks.shape[0], -1) / (pick_sigma * pick_sigma)
-    local_top = jnp.max(score, 1)
-    cell_weights = jnp.exp(score - local_top[:, None])
-    top_score, mass_sum = global_stats(local_top, jnp.sum(cell_weights, 1))
-    scale = jnp.exp(local_top - top_score) / mass_sum
-    density = cell_weights * scale[:, None]
-    density = density.reshape(picks.shape[0], refined.shape[1], refined.shape[2], refined.shape[3])
-    return (refined, density)
+    return refined, event_density(refined, picks, pick_mask)
 
 
 def solution(mesh):

time: 114 us -> 106 us (0.930)
  other arithmetic: 32.7 us -> 0 us
  Pallas kernels: 72.1 us -> 103 us
  local copies, waits for them, and re-layouts: 8.03 us -> 1.84 us
    pallas_call x1 -> x2, Pallas kernels: 17.7 us -> 47.8 us  [the longest x1 44 us: event_density(): pl.pallas_call(locate_kernel, out_shape=(jax.ShapeDtypeStruct((rows,) + w...]
    reduce_sum x25 -> x0, other arithmetic: 26 us -> none  [the longest x8 14 us: misfit_block(): return jnp.sum(observed[:, :, None] * deviation * deviation, 1)]
    mul x1 -> x0, other arithmetic: 3.58 us -> none  [body(): density = cell_weights * scale[:, None]]
    div x1 -> x0, local copies, waits for them, and re-layouts: 1.97 us -> none  [body(): -0.5 * blocks.reshape(picks.shape[0], -1) / (pick_sigma * pick_sigma)]
    div x9 -> x0, other arithmetic: 1.55 us -> none  [the longest x8 0.79 us: misfit_block(): jnp.sum(observed[:, :, None] * residual, 1) / pick_count[:, None]]
    unnamed x7 -> x3, local copies, waits for them, and re-layouts: 2.16 us -> 0.67 us
where the time goes in v3:
time: 106 us; the launch traced here: 105 us
  Pallas kernels  103 us (97%)
  local copies, waits for them, and re-layouts  1.84 us (2%)
    pallas_call x1, Pallas kernels, refined_tables(): pl.pallas_call(travel_kernel, out_shape=jax.ShapeDtypeStruct((stations, d...  53.5 us
    pallas_call x1, Pallas kernels, event_density(): pl.pallas_call(locate_kernel, out_shape=(jax.ShapeDtypeStruct((rows,) + w...  44 us
    pallas_call x1, Pallas kernels, event_density(): pl.pallas_call(density_kernel, out_shape=jax.ShapeDtypeStruct((events * r...  3.79 us

profile of v3, /device:TPU:1, one launch (start us, length us, event | category | flops | bytes accessed | tf_op | source)
XLA Modules:
  0.0 105.4 jit_solution(417744907888653298)
XLA Ops:
  0.6 1.2 %pad_bitcast_fusion.table_ref = f32[1,128]{1,0:T(1,128)} fusion(f32[64]{0:T(128)} %param.7), kind=kLoop, calls=%fused_computation | loop fusion | bytes 768 | tf_op jit(solution)/shard_map/reshape | solution.py:29
  1.8 1.7 %speed.1.speed_ref = f32[5,32,128]{2,1,0:T(8,128)} custom-call(f32[1,128]{1,0:T(1,128)} %pad_bitcast_fusion.table_ref, s32[5,32,128]{2,1,0:T(8,128)} %map_ref.1), custom_call_target="tpu_custom_call" | custom-call | tf_op jit(solution)/shard_map/speed/pallas_call | solution.py:30
  3.5 53.5 %travel.1 = f32[16,5,4,128]{3,2,1,0:T(4,128)} custom-call(f32[2,5,32,128]{3,2,1,0:T(8,128)} %times_ref.1, f32[5,32,128]{2,1,0:T(8,128)} %speed.1.speed_ref), custom_call_target="tpu_custom_call" | custom-call | tf_op jit(solution)/shard_map/travel/pallas_call | solution.py:336
  56.9 44.0 %locate.1 = (f32[20,256,128]{2,1,0:T(8,128)}, f32[256,128]{1,0:T(8,128)}, f32[4,128]{1,0:T(4,128)}) custom-call(f32[320,128]{1,0:T(8,128)} %bitcast.7, f32[16,256]{1,0:T(8,128)} %bitcast.8, s32[16,256]{1,0:T(8,128)} %bitcast.9), custom_call_target="tpu_custom_call" | custom-call | tf_op jit(solution)/shard_map/locate/pallas_call | solution.py:580
  100.9 0.0 copy-start
  100.9 3.8 %density.1 = f32[5120,128]{1,0:T(8,128)} custom-call(f32[20,256,128]{2,1,0:T(8,128)} %get-tuple-element.5.weight_ref, f32[256,128]{1,0:T(8,128)} %get-tuple-element.6.peak_ref, f32[4,128]{1,0:T(4,128)} %get-tuple-element.7.stats_ref), custom_call_target="tpu_custom_call" | custom-call | tf_op jit(solution)/shard_map/density/pallas_call | solution.py:605
  104.7 0.0 copy-done
  104.7 0.7 copy.8
Async XLA Ops:
  100.9 3.8 %copy-start = (f32[16,5,4,128]{3,2,1,0:T(4,128)S(1)}, f32[16,5,4,128]{3,2,1,0:T(4,128)}, u32[]{:S(2)}) copy-start(f32[16,5,4,128]{3,2,1,0:T(4,128)} %travel.1) | copy-start | bytes 491524

commit v4 on v3

--- a/solution.py
+++ b/solution.py
@@ -1,3 +1,5 @@
+import functools
+
 import jax
 import jax.numpy as jnp
 from jax import lax
@@ -15,25 +17,6 @@
 
 HALO = 4
 PAD = 8
-
-
-def speed_kernel(table_ref, map_ref, out_ref):
-    for plane in range(map_ref.shape[0]):
-        index = map_ref[plane]
-        table = jnp.broadcast_to(table_ref[...], index.shape)
-        out_ref[plane] = grid_step * jnp.take_along_axis(table, index, axis=1)
-
-
-def speed_of(model_map, slowness):
-    lanes = model_map.shape[-1]
-    table = jnp.pad(slowness, (0, lanes - slowness.shape[0])).reshape(1, lanes)
-    return pl.pallas_call(
-        speed_kernel,
-        out_shape=jax.ShapeDtypeStruct(model_map.shape, jnp.float32),
-        in_specs=[pl.BlockSpec(memory_space=pltpu.VMEM)] * 2,
-        out_specs=pl.BlockSpec(memory_space=pltpu.VMEM),
-        name="speed",
-    )(table, model_map)
 
 
 def godunov(near_one, near_two, near_three, speed):
@@ -58,8 +41,10 @@
 
 def travel_kernel(
     times_ref,
+    map_ref,
+    slowness_ref,
+    refined_ref,
     speed_ref,
-    refined_ref,
     tab,
     spd,
     swap_in,
@@ -82,7 +67,7 @@
     lines = lax.axis_size("space") // NEAR
     line = space // NEAR
     half = space % NEAR
-    depth, rows, lanes = speed_ref.shape
+    depth, rows, lanes = map_ref.shape
     own = NEAR * depth
     count = own + 2 * HALO
     piece = stage.shape[2]
@@ -122,6 +107,16 @@
         return carry
 
     lax.fori_loop(0, count, rims, 0)
+
+    def look_up(i, carry):
+        index = map_ref[i]
+        value = jnp.zeros(index.shape, jnp.float32)
+        for level in range(slowness_ref.shape[0]):
+            value = jnp.where(index == level, slowness_ref[level], value)
+        speed_ref[i] = grid_step * value
+        return carry
+
+    lax.fori_loop(0, depth, look_up, 0)
     pl.semaphore_wait(barrier, members - 1 + 2 * NEAR)
 
     away = line + 2 * half - 1
@@ -212,7 +207,7 @@
             store(plane, plane_value(side, plane))
             return carry
 
-        lax.fori_loop(0, total, one, 0)
+        lax.fori_loop(0, total, one, 0, unroll=2)
 
     def into(side):
         def store(plane, value):
@@ -321,7 +316,7 @@
     refined_ref[...] = arrived[...]
 
 
-def refined_tables(coarse_times, speed):
+def refined_tables(coarse_times, model_map, slowness):
     per_device, depth, rows, lanes = coarse_times.shape
     stas = lax.axis_size("sta")
     stations = per_device * stas
@@ -336,9 +331,10 @@
     return pl.pallas_call(
         travel_kernel,
         out_shape=jax.ShapeDtypeStruct((stations, depth, piece, lanes), jnp.float32),
-        in_specs=[vmem, vmem],
+        in_specs=[vmem, vmem, pl.BlockSpec(memory_space=pltpu.SMEM)],
         out_specs=vmem,
         scratch_shapes=[
+            pltpu.VMEM((depth,) + plane, jnp.float32),
             pltpu.VMEM((2, count, rows + 2 * PAD, lanes), jnp.float32),
             pltpu.VMEM((count,) + plane, jnp.float32),
             pltpu.VMEM((depth,) + plane, jnp.float32),
@@ -355,12 +351,13 @@
             dma((NEAR * stas,)),
             dma((stations,)),
         ],
-        compiler_params=pltpu.CompilerParams(collective_id=1, has_side_effects=True),
+        compiler_params=pltpu.CompilerParams(collective_id=1, has_side_effects=True, vmem_limit_bytes=16 << 20),
         name="travel",
-    )(coarse_times, speed)
+    )(coarse_times, model_map, slowness)
 
 
 EVENT_TILE = 8
+ROW_UNROLL = 5
 
 
 def locate_kernel(
@@ -454,26 +451,29 @@
             number = number + seen[s]
             total = total + seen[s] * arrival[s]
 
+        share = 1.0 / number
+        mean = total * share
+
         def row(r, top):
-            shift = (total - picked_sum[r, cut]) / number
-            misfit = None
+            shift = mean - picked_sum[r, cut] * share
+            sums = [None] * 4
             for s in range(stations):
                 time = jnp.broadcast_to(times_ref[pl.ds(s * rows + r, 1)], shape)
                 deviation = (arrival[s] - time) - shift
                 term = seen[s] * (deviation * deviation)
-                misfit = term if misfit is None else misfit + term
+                sums[s % 4] = term if sums[s % 4] is None else sums[s % 4] + term
+            misfit = functools.reduce(jnp.add, [part for part in sums if part is not None])
             value = (-0.5 / (pick_sigma * pick_sigma)) * misfit
             score[r] = value
             return jnp.maximum(top, value)
 
-        top = lax.fori_loop(0, rows, row, jnp.full(shape, -3.0e38, jnp.float32))
-
-        def weigh(r, mass):
+        low = jnp.full(shape, -3.0e38, jnp.float32)
+        top = lax.fori_loop(0, rows, row, low, unroll=ROW_UNROLL)
+        mass = jnp.zeros(shape, jnp.float32)
+        for r in range(rows):
             weight = jnp.exp(score[r] - top)
             weight_ref[r, cut] = weight
-            return mass + weight
-
-        mass = lax.fori_loop(0, rows, weigh, jnp.zeros(shape, jnp.float32))
+            mass = mass + weight
         peak_ref[cut] = top
         lane_mass[cut] = mass
         return carry
@@ -599,7 +599,7 @@
             pltpu.SemaphoreType.DMA((2, longest)),
             pltpu.SemaphoreType.DMA((2, longest)),
         ],
-        compiler_params=pltpu.CompilerParams(collective_id=0, has_side_effects=True),
+        compiler_params=pltpu.CompilerParams(collective_id=0, has_side_effects=True, vmem_limit_bytes=16 << 20),
         name="locate",
     )(refined.reshape(stations * rows, lanes), picks.T, pick_mask.T)
     density = pl.pallas_call(
@@ -612,13 +612,14 @@
             pltpu.VMEM((4, 32 * rows, lanes), f32),
             pltpu.SemaphoreType.DMA((4,)),
         ],
+        compiler_params=pltpu.CompilerParams(vmem_limit_bytes=16 << 20),
         name="density",
     )(weight, peak, stats)
     return density.reshape(events, depth, piece, lanes)
 
 
 def body(coarse_times, model_map, slowness, picks, pick_mask):
-    refined = refined_tables(coarse_times, speed_of(model_map, slowness))
+    refined = refined_tables(coarse_times, model_map, slowness)
     return refined, event_density(refined, picks, pick_mask)
 
 

time: 106 us -> 84.5 us (0.80)
  Pallas kernels: 103 us -> 78.9 us
  local copies, waits for them, and re-layouts: 1.84 us -> 4.55 us
    pallas_call x1, Pallas kernels: 44 us -> 27.1 us  [event_density(): pl.pallas_call(locate_kernel, out_shape=(jax.ShapeDtypeStruct((rows,) + w...]
    unnamed x3 -> x11, local copies, waits for them, and re-layouts: 0.67 us -> 4.55 us
    pallas_call x1, Pallas kernels: 53.5 us -> 49.8 us  [refined_tables(): pl.pallas_call(travel_kernel, out_shape=jax.ShapeDtypeStruct((stations, d...]
    pallas_call x1, Pallas kernels: 3.79 us -> 1.93 us  [event_density(): pl.pallas_call(density_kernel, out_shape=jax.ShapeDtypeStruct((events * r...]
    pallas_call x1 -> x0, Pallas kernels: 1.66 us -> none  [speed_of(): pl.pallas_call(speed_kernel, out_shape=jax.ShapeDtypeStruct(model_map.sha...]
    reshape x1 -> x0, local copies, waits for them, and re-layouts: 1.17 us -> none  [speed_of(): table = jnp.pad(slowness, (0, lanes - slowness.shape[0])).reshape(1, lanes)]
where the time goes in v4:
time: 84.5 us; the launch traced here: 84.1 us
  Pallas kernels  78.9 us (93%)
  local copies, waits for them, and re-layouts  4.55 us (5%)
    pallas_call x1, Pallas kernels, refined_tables(): pl.pallas_call(travel_kernel, out_shape=jax.ShapeDtypeStruct((stations, d...  49.8 us
    pallas_call x1, Pallas kernels, event_density(): pl.pallas_call(locate_kernel, out_shape=(jax.ShapeDtypeStruct((rows,) + w...  27.1 us
    unnamed x11, local copies, waits for them, and re-layouts  4.55 us
    pallas_call x1, Pallas kernels, event_density(): pl.pallas_call(density_kernel, out_shape=jax.ShapeDtypeStruct((events * r...  1.93 us

profile of v4, /device:TPU:1, one launch (start us, length us, event | category | flops | bytes accessed | tf_op | source)
XLA Modules:
  0.0 84.1 jit_solution(1270279512881239443)
XLA Ops:
  0.6 0.0 copy-start
  0.6 0.9 %copy-done = f32[2,5,32,128]{3,2,1,0:T(8,128)S(1)} copy-done((f32[2,5,32,128]{3,2,1,0:T(8,128)S(1)}, f32[2,5,32,128]{3,2,1,0:T(8,128)}, u32[]{:S(2)}) %copy-start) | copy-done | bytes 163864
  1.5 0.0 copy-start.1
  1.5 0.9 %copy-done.1 = s32[5,32,128]{2,1,0:T(8,128)S(1)} copy-done((s32[5,32,128]{2,1,0:T(8,128)S(1)}, s32[5,32,128]{2,1,0:T(8,128)}, u32[]{:S(2)}) %copy-start.1) | copy-done | bytes 81944
  2.4 0.0 copy-start.4
  2.4 0.7 copy-done.4
  3.1 49.8 %travel.1 = f32[16,5,4,128]{3,2,1,0:T(4,128)S(1)} custom-call(f32[2,5,32,128]{3,2,1,0:T(8,128)S(1)} %copy-done, s32[5,32,128]{2,1,0:T(8,128)S(1)} %copy-done.1, f32[64]{0:T(128)S(1)} %copy-done.4), custom_call_target="tpu_custom_call" | custom-call | tf_op jit(solution)/shard_map/travel/pallas_call | solution.py:331
  52.9 0.0 copy-start.2
  52.9 0.7 copy-done.2
  53.7 0.0 copy-start.3
  53.7 0.7 copy-done.3
  54.4 27.1 %locate.1 = (f32[20,256,128]{2,1,0:T(8,128)S(1)}, f32[256,128]{1,0:T(8,128)S(1)}, f32[4,128]{1,0:T(4,128)S(1)}) custom-call(f32[320,128]{1,0:T(8,128)S(1)} %bitcast.4, f32[16,256]{1,0:T(8,128)S(1)} %bitcast.5, s32[16,256]{1,0:T(8,128)S(1)} %bitcast.6), custom_call_target="tpu_custom_call" | custom-call | tf_op jit(solution)/shard_map/locate/pallas_call | solution.py:580
  81.5 1.9 %density.1 = f32[5120,128]{1,0:T(8,128)} custom-call(f32[20,256,128]{2,1,0:T(8,128)S(1)} %get-tuple-element.5.weight_ref, f32[256,128]{1,0:T(8,128)S(1)} %get-tuple-element.6.peak_ref, f32[4,128]{1,0:T(4,128)S(1)} %get-tuple-element.7.stats_ref), custom_call_target="tpu_custom_call" | custom-call | tf_op jit(solution)/shard_map/density/pallas_call | solution.py:605
  83.4 0.7 copy.8
Async XLA Ops:
  0.6 0.9 %copy-start = (f32[2,5,32,128]{3,2,1,0:T(8,128)S(1)}, f32[2,5,32,128]{3,2,1,0:T(8,128)}, u32[]{:S(2)}) copy-start(f32[2,5,32,128]{3,2,1,0:T(8,128)} %times_ref.1) | copy-start | bytes 491524
  1.5 0.9 %copy-start.1 = (s32[5,32,128]{2,1,0:T(8,128)S(1)}, s32[5,32,128]{2,1,0:T(8,128)}, u32[]{:S(2)}) copy-start(s32[5,32,128]{2,1,0:T(8,128)} %map_ref.1) | copy-start | bytes 245764
  2.4 0.7 copy-start.4
  52.9 0.7 copy-start.2
  53.7 0.7 copy-start.3

commit v5 on v4

--- a/solution.py
+++ b/solution.py
@@ -39,11 +39,34 @@
     return lowest + jnp.where(speed <= gap_mid, speed, steep)
 
 
+def event_rows(picks_ref, mask_ref, pick_rows, mask_rows):
+    stations, events = picks_ref.shape
+    lanes = pick_rows.shape[1]
+    for b in range(events // lanes):
+        cut = pl.ds(b * lanes, lanes)
+        part = picks_ref[:, cut]
+        blank = jnp.zeros((lanes - stations, lanes), jnp.float32)
+        pick_rows[cut] = jnp.concatenate([part, blank], 0).T
+        part = mask_ref[:, cut].astype(jnp.float32)
+        blank = jnp.zeros((lanes - 3 * stations, lanes), jnp.float32)
+        mask_rows[cut] = jnp.concatenate([part, part, part, blank], 0).T
+
+
 def travel_kernel(
     times_ref,
+    map_hbm,
+    slowness_hbm,
+    picks_hbm,
+    mask_hbm,
+    refined_ref,
+    pick_rows,
+    mask_rows,
+    own_times,
     map_ref,
     slowness_ref,
-    refined_ref,
+    picks_ref,
+    mask_ref,
+    load_sem,
     speed_ref,
     tab,
     spd,
@@ -77,6 +100,21 @@
     inside = pl.ds(PAD, rows)
     mesh_id = pl.DeviceIdType.MESH
 
+    loads = [
+        pltpu.make_async_copy(src, dst, load_sem.at[i])
+        for i, (src, dst) in enumerate(
+            (
+                (map_hbm, map_ref),
+                (slowness_hbm, slowness_ref),
+                (times_ref.at[half], own_times),
+                (picks_hbm, picks_ref),
+                (mask_hbm, mask_ref),
+            )
+        )
+    ]
+    for load in loads:
+        load.start()
+
     def at(other_line, other_half):
         return {"space": ((other_line + lines) % lines) * NEAR + other_half, "sta": sta}
 
@@ -116,6 +154,8 @@
         speed_ref[i] = grid_step * value
         return carry
 
+    loads[0].wait()
+    loads[1].wait()
     lax.fori_loop(0, depth, look_up, 0)
     pl.semaphore_wait(barrier, members - 1 + 2 * NEAR)
 
@@ -161,30 +201,29 @@
             device_id_type=mesh_id,
         )
 
-    for j in (2, 3, 0, 4, 5, 1):
+    for j in (0, 2, 3, 1, 4, 5):
         start_copy(j).start()
 
     at_lower = line == 0
     at_upper = line == lines - 1
 
+    loads[3].wait()
+    loads[4].wait()
+    event_rows(picks_ref, mask_ref, pick_rows, mask_rows)
+    loads[2].wait()
     for i in range(depth):
-        tab[0, HALO + half * depth + i, inside] = times_ref[half, i]
+        tab[0, HALO + half * depth + i, inside] = own_times[i]
         spd[HALO + half * depth + i] = speed_ref[i]
-    for slot in range(6):
+    for slot in range(2):
         start_arrival(slot).wait_recv()
     for i in range(depth):
         tab[0, HALO + (1 - half) * depth + i, inside] = swap_in[i]
         spd[HALO + (1 - half) * depth + i] = swap_speed[i]
-    for i in range(HALO):
-        spd[i] = halo_speed[0, i]
-        spd[HALO + own + i] = halo_speed[1, i]
 
     def place_halo(exchange, side):
         for i in range(HALO):
             tab[side, i, inside] = jnp.where(at_lower, BIG, halo_in[exchange, 0, i])
             tab[side, HALO + own + i, inside] = jnp.where(at_upper, BIG, halo_in[exchange, 1, i])
-
-    place_halo(0, 0)
 
     lane = lax.broadcasted_iota(jnp.int32, (rows, lanes), 1)
 
@@ -249,27 +288,29 @@
     side = 0
     for exchange in range(exchanges):
         final = exchange == exchanges - 1
+        start = side
+        for r in range(HALO - 1):
+            sweep(side, own - 2 - 2 * r, lambda j, r=r: HALO + 1 + r + j, into(1 - side))
+            side = 1 - side
         if exchange == 0:
-            for r in range(HALO - 1):
-                sweep(side, count - 2 - 2 * r, lambda j, r=r: r + 1 + j, into(1 - side))
-                side = 1 - side
+            for slot in range(2, 6):
+                start_arrival(slot).wait_recv()
+            for i in range(HALO):
+                spd[i] = halo_speed[0, i]
+                spd[HALO + own + i] = halo_speed[1, i]
         else:
-            start = side
-            for r in range(HALO - 1):
-                sweep(side, own - 2 - 2 * r, lambda j, r=r: HALO + 1 + r + j, into(1 - side))
-                side = 1 - side
             for lower in (True, False):
                 halo_copy(exchange, lower).wait()
-            side = start
-            place_halo(exchange, side)
-            for r in range(HALO - 1):
-                sweep(
-                    side,
-                    2 * HALO,
-                    lambda j, r=r: jnp.where(j < HALO, r + 1 + j, own - 1 - r + j),
-                    into(1 - side),
-                )
-                side = 1 - side
+        side = start
+        place_halo(exchange, side)
+        for r in range(HALO - 1):
+            sweep(
+                side,
+                2 * HALO,
+                lambda j, r=r: jnp.where(j < HALO, r + 1 + j, own - 1 - r + j),
+                into(1 - side),
+            )
+            side = 1 - side
         if final:
             sweep(side, own, lambda j: HALO + j, into_stage)
         else:
@@ -316,7 +357,7 @@
     refined_ref[...] = arrived[...]
 
 
-def refined_tables(coarse_times, model_map, slowness):
+def refined_tables(coarse_times, model_map, slowness, picks, pick_mask):
     per_device, depth, rows, lanes = coarse_times.shape
     stas = lax.axis_size("sta")
     stations = per_device * stas
@@ -328,12 +369,25 @@
     plane = (rows, lanes)
     vmem = pl.BlockSpec(memory_space=pltpu.VMEM)
     dma = pltpu.SemaphoreType.DMA
+    events = picks.shape[0]
+    wide = (events, lanes)
+    hbm = pl.BlockSpec(memory_space=pltpu.HBM)
     return pl.pallas_call(
         travel_kernel,
-        out_shape=jax.ShapeDtypeStruct((stations, depth, piece, lanes), jnp.float32),
-        in_specs=[vmem, vmem, pl.BlockSpec(memory_space=pltpu.SMEM)],
-        out_specs=vmem,
+        out_shape=(
+            jax.ShapeDtypeStruct((stations, depth, piece, lanes), jnp.float32),
+            jax.ShapeDtypeStruct(wide, jnp.float32),
+            jax.ShapeDtypeStruct(wide, jnp.float32),
+        ),
+        in_specs=[hbm] * 5,
+        out_specs=[vmem] * 3,
         scratch_shapes=[
+            pltpu.VMEM((depth,) + plane, jnp.float32),
+            pltpu.VMEM((depth,) + plane, jnp.int32),
+            pltpu.SMEM(slowness.shape, jnp.float32),
+            pltpu.VMEM((stations, events), jnp.float32),
+            pltpu.VMEM((stations, events), jnp.int32),
+            dma((5,)),
             pltpu.VMEM((depth,) + plane, jnp.float32),
             pltpu.VMEM((2, count, rows + 2 * PAD, lanes), jnp.float32),
             pltpu.VMEM((count,) + plane, jnp.float32),
@@ -353,7 +407,7 @@
         ],
         compiler_params=pltpu.CompilerParams(collective_id=1, has_side_effects=True, vmem_limit_bytes=16 << 20),
         name="travel",
-    )(coarse_times, model_map, slowness)
+    )(*[pltpu.with_memory_space_constraint(x, pltpu.HBM) for x in (coarse_times, model_map, slowness, picks.T, pick_mask.T)])
 
 
 EVENT_TILE = 8
@@ -362,13 +416,11 @@
 
 def locate_kernel(
     times_ref,
-    picks_ref,
-    mask_ref,
+    pick_rows,
+    mask_rows,
     weight_ref,
     peak_ref,
     stats_ref,
-    pick_rows,
-    mask_rows,
     picked_sum,
     score,
     lane_mass,
@@ -406,18 +458,9 @@
     greet(member_id, members)
     greet(line_id, lines)
 
-    stations, events = picks_ref.shape
-    rows, _, lanes = weight_ref.shape
+    rows, events, lanes = weight_ref.shape
+    stations = times_ref.shape[0] // rows
     blocks = events // lanes
-
-    for b in range(blocks):
-        cut = pl.ds(b * lanes, lanes)
-        part = picks_ref[:, cut]
-        blank = jnp.zeros((lanes - stations, lanes), jnp.float32)
-        pick_rows[cut] = jnp.concatenate([part, blank], 0).T
-        part = mask_ref[:, cut].astype(jnp.float32)
-        blank = jnp.zeros((lanes - 3 * stations, lanes), jnp.float32)
-        mask_rows[cut] = jnp.concatenate([part, part, part, blank], 0).T
 
     chosen = mask_rows[...].astype(jnp.bfloat16)
     blank = jnp.zeros((lanes - 3 * stations, lanes), jnp.float32)
@@ -531,7 +574,11 @@
     stats_ref[blocks:] = mass
 
 
-def density_kernel(weight_ref, peak_ref, stats_ref, out_ref, scale, chunk, sem):
+def density_kernel(
+    weight_ref, peak_ref, stats_ref, refined_ref, out_ref, table_ref, scale, chunk, sem, table_sem
+):
+    table = pltpu.make_async_copy(refined_ref, table_ref, table_sem)
+    table.start()
     rows, events, lanes = weight_ref.shape
     blocks = events // lanes
     size = chunk.shape[1] // rows
@@ -562,11 +609,12 @@
         copy(c, slot).start()
     for c in range(chunks - slots, chunks):
         copy(c, c % slots).wait()
-
-
-def event_density(refined, picks, pick_mask):
+    table.wait()
+
+
+def event_density(refined, pick_rows, mask_rows):
     stations, depth, piece, lanes = refined.shape
-    events = picks.shape[0]
+    events = pick_rows.shape[0]
     rows = depth * piece
     assert 3 * stations <= lanes and events % lanes == 0 and rows % 2 == 0
     blocks = events // lanes
@@ -587,8 +635,6 @@
         in_specs=[vmem] * 3,
         out_specs=[vmem] * 3,
         scratch_shapes=[
-            pltpu.VMEM(wide, f32),
-            pltpu.VMEM(wide, f32),
             pltpu.VMEM((rows,) + wide, f32),
             pltpu.VMEM((rows, EVENT_TILE, lanes), f32),
             pltpu.VMEM(wide, f32),
@@ -601,26 +647,32 @@
         ],
         compiler_params=pltpu.CompilerParams(collective_id=0, has_side_effects=True, vmem_limit_bytes=16 << 20),
         name="locate",
-    )(refined.reshape(stations * rows, lanes), picks.T, pick_mask.T)
-    density = pl.pallas_call(
+    )(refined.reshape(stations * rows, lanes), pick_rows, mask_rows)
+    density, table = pl.pallas_call(
         density_kernel,
-        out_shape=jax.ShapeDtypeStruct((events * rows, lanes), f32),
-        in_specs=[vmem] * 3,
-        out_specs=pl.BlockSpec(memory_space=pl.ANY),
+        out_shape=(
+            jax.ShapeDtypeStruct((events * rows, lanes), f32),
+            jax.ShapeDtypeStruct(refined.shape, f32),
+        ),
+        in_specs=[vmem] * 4,
+        out_specs=[pl.BlockSpec(memory_space=pltpu.HBM)] * 2,
         scratch_shapes=[
             pltpu.VMEM(wide, f32),
             pltpu.VMEM((4, 32 * rows, lanes), f32),
             pltpu.SemaphoreType.DMA((4,)),
+            pltpu.SemaphoreType.DMA,
         ],
         compiler_params=pltpu.CompilerParams(vmem_limit_bytes=16 << 20),
         name="density",
-    )(weight, peak, stats)
-    return density.reshape(events, depth, piece, lanes)
+    )(weight, peak, stats, refined)
+    return table, density.reshape(events, depth, piece, lanes)
 
 
 def body(coarse_times, model_map, slowness, picks, pick_mask):
-    refined = refined_tables(coarse_times, model_map, slowness)
-    return refined, event_density(refined, picks, pick_mask)
+    refined, pick_rows, mask_rows = refined_tables(
+        coarse_times, model_map, slowness, picks, pick_mask
+    )
+    return event_density(refined, pick_rows, mask_rows)
 
 
 def solution(mesh):

time: 84.5 us -> 79.8 us (0.944)
  local copies, waits for them, and re-layouts: 4.55 us -> 0 us
    unnamed x11 -> x0, local copies, waits for them, and re-layouts: 4.55 us -> none
where the time goes in v5:
time: 79.8 us; the launch traced here: 79.6 us
  Pallas kernels  78.9 us (99%)
    pallas_call x1, Pallas kernels, refined_tables(): pl.pallas_call(travel_kernel, out_shape=(jax.ShapeDtypeStruct((stations,...  50.5 us
    pallas_call x1, Pallas kernels, event_density(): pl.pallas_call(locate_kernel, out_shape=(jax.ShapeDtypeStruct((rows,) + w...  26.5 us
    pallas_call x1, Pallas kernels, event_density(): pl.pallas_call(density_kernel, out_shape=(jax.ShapeDtypeStruct((events *...  1.94 us

profile of v5, /device:TPU:1, one launch (start us, length us, event | category | flops | bytes accessed | tf_op | source)
XLA Modules:
  0.0 79.6 jit_solution(15735185869426915626)
XLA Ops:
  0.6 50.5 %travel.1 = (f32[16,5,4,128]{3,2,1,0:T(4,128)S(1)}, f32[256,128]{1,0:T(8,128)S(1)}, f32[256,128]{1,0:T(8,128)S(1)}) custom-call(f32[2,5,32,128]{3,2,1,0:T(8,128)} %times_ref.1, s32[5,32,128]{2,1,0:T(8,128)} %map_hbm.1, f32[64]{0:T(128)} %slowness_hbm.1, f32[16,256]{1,0:T(8,128)} %bitcast.5, s32[16,256]{1,0:T(8,128)} %bitcast.6), custom_call_target="tpu_custom_call" | custom-call | tf_op jit(solution)/shard_map/travel/pallas_call | solution.py:375
  51.1 26.5 %locate.1 = (f32[20,256,128]{2,1,0:T(8,128)S(1)}, f32[256,128]{1,0:T(8,128)S(1)}, f32[4,128]{1,0:T(4,128)S(1)}) custom-call(f32[320,128]{1,0:T(8,128)S(1)} %bitcast.4, f32[256,128]{1,0:T(8,128)S(1)} %get-tuple-element.11.pick_rows, f32[256,128]{1,0:T(8,128)S(1)} %get-tuple-element.12.mask_rows), custom_call_target="tpu_custom_call" | custom-call | tf_op jit(solution)/shard_map/locate/pallas_call | solution.py:628
  77.6 1.9 %density.1 = (f32[5120,128]{1,0:T(8,128)}, f32[16,5,4,128]{3,2,1,0:T(4,128)}) custom-call(f32[20,256,128]{2,1,0:T(8,128)S(1)} %get-tuple-element.13.weight_ref, f32[256,128]{1,0:T(8,128)S(1)} %get-tuple-element.14.peak_ref, f32[4,128]{1,0:T(4,128)S(1)} %get-tuple-element.15.stats_ref, f32[16,5,4,128]{3,2,1,0:T(4,128)S(1)} %get-tuple-element.10.refined_ref), custom_call_target="tpu_custom_call" | custom-call | tf_op jit(solution)/shard_map/density/pallas_call | solution.py:651

commit v6 on v5

--- a/solution.py
+++ b/solution.py
@@ -17,6 +17,8 @@
 
 HALO = 4
 PAD = 8
+EVENT_TILE = 8
+ROW_UNROLL = 5
 
 
 def godunov(near_one, near_two, near_three, speed):
@@ -29,13 +31,12 @@
     gap_high = highest - lowest
     spread = highest - middle
     square = speed * speed
-    mid_square = gap_mid * gap_mid
-    reach = gap_high * gap_high + spread * spread
-    two = square <= reach
-    inner = jnp.where(two, 2.0 * square, 3.0 * square - reach) - mid_square
-    root = jnp.sqrt(jnp.maximum(inner, 0.0))
-    base = gap_mid + jnp.where(two, 0.0, gap_high)
-    steep = (base + root) * jnp.where(two, 0.5, 1.0 / 3.0)
+    excess = square - (gap_high * gap_high + spread * spread)
+    two = excess <= 0.0
+    inner = (square + square - gap_mid * gap_mid) + jnp.maximum(excess, 0.0)
+    inner = jnp.maximum(inner, 1e-30)
+    base = gap_mid + inner * lax.rsqrt(inner)
+    steep = jnp.where(two, 0.5 * base, (base + gap_high) * (1.0 / 3.0))
     return lowest + jnp.where(speed <= gap_mid, speed, steep)
 
 
@@ -52,6 +53,30 @@
         mask_rows[cut] = jnp.concatenate([part, part, part, blank], 0).T
 
 
+def spread_events(stations, pick_rows, mask_rows, arrival_ref, seen_ref, mean_ref, share_ref):
+    events, lanes = pick_rows.shape
+    shape = (EVENT_TILE, lanes)
+
+    def tile(index, carry):
+        cut = pl.ds(pl.multiple_of(index * EVENT_TILE, EVENT_TILE), EVENT_TILE)
+        pick = pick_rows[cut]
+        mask = mask_rows[cut]
+        number = None
+        for s in range(stations):
+            arrival = jnp.broadcast_to(pick[:, s : s + 1], shape)
+            seen = jnp.broadcast_to(mask[:, s : s + 1], shape)
+            arrival_ref[s, cut] = arrival
+            seen_ref[s, cut] = seen
+            number = seen if number is None else number + seen
+            total = seen * arrival if s == 0 else total + seen * arrival
+        share = 1.0 / number
+        mean_ref[cut] = total * share
+        share_ref[cut] = share
+        return carry
+
+    lax.fori_loop(0, events // EVENT_TILE, tile, 0)
+
+
 def travel_kernel(
     times_ref,
     map_hbm,
@@ -59,8 +84,12 @@
     picks_hbm,
     mask_hbm,
     refined_ref,
+    mask_rows,
+    arrival_ref,
+    seen_ref,
+    mean_ref,
+    share_ref,
     pick_rows,
-    mask_rows,
     own_times,
     map_ref,
     slowness_ref,
@@ -210,6 +239,9 @@
     loads[3].wait()
     loads[4].wait()
     event_rows(picks_ref, mask_ref, pick_rows, mask_rows)
+    spread_events(
+        picks_ref.shape[0], pick_rows, mask_rows, arrival_ref, seen_ref, mean_ref, share_ref
+    )
     loads[2].wait()
     for i in range(depth):
         tab[0, HALO + half * depth + i, inside] = own_times[i]
@@ -227,7 +259,7 @@
 
     lane = lax.broadcasted_iota(jnp.int32, (rows, lanes), 1)
 
-    def plane_value(side, plane):
+    def plane_value(side, plane, ghost):
         centre = tab[side, plane, inside]
         along_x = jnp.minimum(tab[side, plane - 1, inside], tab[side, plane + 1, inside])
         along_y = jnp.minimum(
@@ -237,16 +269,26 @@
         after = jnp.where(lane == lanes - 1, BIG, pltpu.roll(centre, lanes - 1, 1))
         along_z = jnp.minimum(before, after)
         value = jnp.minimum(centre, godunov(along_x, along_y, along_z, spd[plane]))
+        if not ghost:
+            return value
         outside = (at_lower & (plane < HALO)) | (at_upper & (plane >= HALO + own))
         return jnp.maximum(value, jnp.where(outside, BIG, -BIG))
 
-    def sweep(side, total, plane_at, store):
+    def sweep(side, total, first, store):
         def one(j, carry):
-            plane = plane_at(j)
-            store(plane, plane_value(side, plane))
+            store(first + j, plane_value(side, first + j, False))
             return carry
 
-        lax.fori_loop(0, total, one, 0, unroll=2)
+        unroll = next(u for u in (4, 5, 3, 2, 1) if total % u == 0)
+        lax.fori_loop(0, total, one, 0, unroll=unroll)
+
+    def sweep_edges(side, done):
+        def one(j, carry):
+            for plane in (done + 1 + j, HALO + own - 1 - done + j):
+                tab[1 - side, plane, inside] = plane_value(side, plane, True)
+            return carry
+
+        lax.fori_loop(0, HALO, one, 0, unroll=2)
 
     def into(side):
         def store(plane, value):
@@ -278,11 +320,11 @@
         )
 
     def last_round(side, exchange):
-        sweep(side, HALO, lambda j: HALO + j, into_edge(1 - side, exchange - 1, True))
+        sweep(side, HALO, HALO, into_edge(1 - side, exchange - 1, True))
         halo_copy(exchange, True).start()
-        sweep(side, HALO, lambda j: own + j, into_edge(1 - side, exchange - 1, False))
+        sweep(side, HALO, own, into_edge(1 - side, exchange - 1, False))
         halo_copy(exchange, False).start()
-        sweep(side, own - 2 * HALO, lambda j: 2 * HALO + j, into(1 - side))
+        sweep(side, own - 2 * HALO, 2 * HALO, into(1 - side))
 
     exchanges = ROUNDS // HALO
     side = 0
@@ -290,7 +332,7 @@
         final = exchange == exchanges - 1
         start = side
         for r in range(HALO - 1):
-            sweep(side, own - 2 - 2 * r, lambda j, r=r: HALO + 1 + r + j, into(1 - side))
+            sweep(side, own - 2 - 2 * r, HALO + 1 + r, into(1 - side))
             side = 1 - side
         if exchange == 0:
             for slot in range(2, 6):
@@ -304,15 +346,10 @@
         side = start
         place_halo(exchange, side)
         for r in range(HALO - 1):
-            sweep(
-                side,
-                2 * HALO,
-                lambda j, r=r: jnp.where(j < HALO, r + 1 + j, own - 1 - r + j),
-                into(1 - side),
-            )
+            sweep_edges(side, r)
             side = 1 - side
         if final:
-            sweep(side, own, lambda j: HALO + j, into_stage)
+            sweep(side, own, HALO, into_stage)
         else:
             last_round(side, exchange + 1)
             side = 1 - side
@@ -377,11 +414,15 @@
         out_shape=(
             jax.ShapeDtypeStruct((stations, depth, piece, lanes), jnp.float32),
             jax.ShapeDtypeStruct(wide, jnp.float32),
+            jax.ShapeDtypeStruct((stations,) + wide, jnp.float32),
+            jax.ShapeDtypeStruct((stations,) + wide, jnp.float32),
+            jax.ShapeDtypeStruct(wide, jnp.float32),
             jax.ShapeDtypeStruct(wide, jnp.float32),
         ),
         in_specs=[hbm] * 5,
-        out_specs=[vmem] * 3,
+        out_specs=[vmem] * 6,
         scratch_shapes=[
+            pltpu.VMEM(wide, jnp.float32),
             pltpu.VMEM((depth,) + plane, jnp.float32),
             pltpu.VMEM((depth,) + plane, jnp.int32),
             pltpu.SMEM(slowness.shape, jnp.float32),
@@ -410,14 +451,13 @@
     )(*[pltpu.with_memory_space_constraint(x, pltpu.HBM) for x in (coarse_times, model_map, slowness, picks.T, pick_mask.T)])
 
 
-EVENT_TILE = 8
-ROW_UNROLL = 5
-
-
 def locate_kernel(
     times_ref,
-    pick_rows,
     mask_rows,
+    arrival_ref,
+    seen_ref,
+    mean_ref,
+    share_ref,
     weight_ref,
     peak_ref,
     stats_ref,
@@ -484,18 +524,10 @@
     def tile(index, carry):
         cut = pl.ds(pl.multiple_of(index * EVENT_TILE, EVENT_TILE), EVENT_TILE)
         shape = (EVENT_TILE, lanes)
-        pick = pick_rows[cut]
-        mask = mask_rows[cut]
-        arrival = [jnp.broadcast_to(pick[:, s : s + 1], shape) for s in range(stations)]
-        seen = [jnp.broadcast_to(mask[:, s : s + 1], shape) for s in range(stations)]
-        number = seen[0]
-        total = seen[0] * arrival[0]
-        for s in range(1, stations):
-            number = number + seen[s]
-            total = total + seen[s] * arrival[s]
-
-        share = 1.0 / number
-        mean = total * share
+        arrival = [arrival_ref[s, cut] for s in range(stations)]
+        seen = [seen_ref[s, cut] for s in range(stations)]
+        mean = mean_ref[cut]
+        share = share_ref[cut]
 
         def row(r, top):
             shift = mean - picked_sum[r, cut] * share
@@ -552,7 +584,8 @@
             copy(k).wait()
             return carry
 
-        lax.fori_loop(1, count, start, 0)
+        lax.fori_loop(count // 4, count, start, 0)
+        lax.fori_loop(1, count // 4, start, 0)
         lax.fori_loop(1, count, wait, 0)
 
     def merged(top, mass, slots, count):
@@ -612,9 +645,9 @@
     table.wait()
 
 
-def event_density(refined, pick_rows, mask_rows):
+def event_density(refined, mask_rows, *events_over_lanes):
     stations, depth, piece, lanes = refined.shape
-    events = pick_rows.shape[0]
+    events = mask_rows.shape[0]
     rows = depth * piece
     assert 3 * stations <= lanes and events % lanes == 0 and rows % 2 == 0
     blocks = events // lanes
@@ -632,7 +665,7 @@
             jax.ShapeDtypeStruct(wide, f32),
             jax.ShapeDtypeStruct(message, f32),
         ),
-        in_specs=[vmem] * 3,
+        in_specs=[vmem] * 6,
         out_specs=[vmem] * 3,
         scratch_shapes=[
             pltpu.VMEM((rows,) + wide, f32),
@@ -647,7 +680,7 @@
         ],
         compiler_params=pltpu.CompilerParams(collective_id=0, has_side_effects=True, vmem_limit_bytes=16 << 20),
         name="locate",
-    )(refined.reshape(stations * rows, lanes), pick_rows, mask_rows)
+    )(refined.reshape(stations * rows, lanes), mask_rows, *events_over_lanes)
     density, table = pl.pallas_call(
         density_kernel,
         out_shape=(
@@ -669,10 +702,8 @@
 
 
 def body(coarse_times, model_map, slowness, picks, pick_mask):
-    refined, pick_rows, mask_rows = refined_tables(
-        coarse_times, model_map, slowness, picks, pick_mask
-    )
-    return event_density(refined, pick_rows, mask_rows)
+    refined, *events = refined_tables(coarse_times, model_map, slowness, picks, pick_mask)
+    return event_density(refined, *events)
 
 
 def solution(mesh):

time: 79.8 us -> 71 us (0.89)
  Pallas kernels: 78.9 us -> 70.2 us
    pallas_call x1, Pallas kernels: 50.5 us -> 45.2 us  [refined_tables(): pl.pallas_call(travel_kernel, out_shape=(jax.ShapeDtypeStruct((stations,...]
    pallas_call x1, Pallas kernels: 26.5 us -> 23.1 us  [event_density(): pl.pallas_call(locate_kernel, out_shape=(jax.ShapeDtypeStruct((rows,) + w...]
where the time goes in v6:
time: 71 us; the launch traced here: 70.8 us
  Pallas kernels  70.2 us (99%)
    pallas_call x1, Pallas kernels, refined_tables(): pl.pallas_call(travel_kernel, out_shape=(jax.ShapeDtypeStruct((stations,...  45.2 us
    pallas_call x1, Pallas kernels, event_density(): pl.pallas_call(locate_kernel, out_shape=(jax.ShapeDtypeStruct((rows,) + w...  23.1 us
    pallas_call x1, Pallas kernels, event_density(): pl.pallas_call(density_kernel, out_shape=(jax.ShapeDtypeStruct((events *...  1.94 us

profile of v6, /device:TPU:1, one launch (start us, length us, event | category | flops | bytes accessed | tf_op | source)
XLA Modules:
  0.0 70.8 jit_solution(7382612783830269009)
XLA Ops:
  0.6 45.2 %travel.1 = (f32[16,5,4,128]{3,2,1,0:T(4,128)S(1)}, f32[256,128]{1,0:T(8,128)S(1)}, f32[16,256,128]{2,1,0:T(8,128)S(1)}, f32[16,256,128]{2,1,0:T(8,128)S(1)}, f3...) custom-call(f32[2,5,32,128]{3,2,1,0:T(8,128)} %times_ref.1, s32[5,32,128]{2,1,0:T(8,128)} %map_hbm.1, f32[64]{0:T(128)} %slowness_hbm.1, ...), custom_call_target="tpu_custom_call" | custom-call | tf_op jit(solution)/shard_map/travel/pallas_call | solution.py:412
  45.8 23.1 %locate.1 = (f32[20,256,128]{2,1,0:T(8,128)S(1)}, f32[256,128]{1,0:T(8,128)S(1)}, f32[4,128]{1,0:T(4,128)S(1)}) custom-call(f32[320,128]{1,0:T(8,128)S(1)} %bitcast.4, f32[256,128]{1,0:T(8,128)S(1)} %get-tuple-element.14.mask_rows, f32[16,256,128]{2,1,0:T(8,128)S(1)} %get-tuple-element.15.arrival_ref, f32[16,256,128]{2,1,0:T(8,128)S(1)} %get-tuple-element.16.seen_ref, ...), custom_call_target="tpu_custom_call" | custom-call | tf_op jit(solution)/shard_map/locate/pallas_call | solution.py:661
  68.9 1.9 %density.1 = (f32[5120,128]{1,0:T(8,128)}, f32[16,5,4,128]{3,2,1,0:T(4,128)}) custom-call(f32[20,256,128]{2,1,0:T(8,128)S(1)} %get-tuple-element.19.weight_ref, f32[256,128]{1,0:T(8,128)S(1)} %get-tuple-element.20.peak_ref, f32[4,128]{1,0:T(4,128)S(1)} %get-tuple-element.21.stats_ref, f32[16,5,4,128]{3,2,1,0:T(4,128)S(1)} %get-tuple-element.13.refined_ref), custom_call_target="tpu_custom_call" | custom-call | tf_op jit(solution)/shard_map/density/pallas_call | solution.py:684

commit v7 on v6

--- a/solution.py
+++ b/solution.py
@@ -15,7 +15,7 @@
 NEAR = 2
 
 
-HALO = 4
+BLOCKS = (4, 8)
 PAD = 8
 EVENT_TILE = 8
 ROW_UNROLL = 5
@@ -101,8 +101,11 @@
     spd,
     swap_in,
     swap_speed,
-    halo_in,
-    halo_speed,
+    halo_first,
+    halo_next,
+    near_speed,
+    rest_speed,
+    far_speed,
     edge_out,
     stage,
     arrived,
@@ -121,7 +124,9 @@
     half = space % NEAR
     depth, rows, lanes = map_ref.shape
     own = NEAR * depth
-    count = own + 2 * HALO
+    near, ghost = BLOCKS
+    far = ghost - depth
+    count = own + 2 * ghost
     piece = stage.shape[2]
     member = half * stas + sta
     members = NEAR * stas
@@ -189,20 +194,25 @@
     pl.semaphore_wait(barrier, members - 1 + 2 * NEAR)
 
     away = line + 2 * half - 1
-    first = half * (depth - HALO)
+    back = line - 2 * half + 1
 
     def start_copy(j):
-        if j == 0:
-            src, dst, who = times_ref.at[1 - half], swap_in, at(line, 1 - half)
-        elif j == 1:
-            src, dst, who = speed_ref, swap_speed, at(line, 1 - half)
-        elif j < 4:
-            src = times_ref.at[j - 2, pl.ds(first, HALO)]
-            dst, who = halo_in.at[0, 1 - half], at(away, j - 2)
+        kind, other = j // 2, j % 2
+        if kind == 0:
+            src, dst = ((times_ref.at[1 - half], swap_in), (speed_ref, swap_speed))[other]
+            who, slot = at(line, 1 - half), other
+        elif kind == 1:
+            src = times_ref.at[other, pl.ds(half * (depth - near), near)]
+            dst, who, slot = halo_first.at[1 - half], at(away, other), 2 + (1 - half)
+        elif kind == 2:
+            src = speed_ref.at[pl.ds(half * (depth - near), near)]
+            dst, who, slot = near_speed.at[1 - half], at(away, other), 4 + (1 - half)
+        elif kind == 3:
+            src = speed_ref.at[pl.ds((1 - half) * near, depth - near)]
+            dst, who, slot = rest_speed.at[1 - half], at(away, other), 6 + (1 - half)
         else:
-            src = speed_ref.at[pl.ds(first, HALO)]
-            dst, who = halo_speed.at[1 - half], at(away, j - 4)
-        slot = j if j < 2 else (2 if j < 4 else 4) + (1 - half)
+            src = speed_ref.at[pl.ds((1 - half) * (depth - far), far)]
+            dst, who, slot = far_speed.at[half], at(back, other), 8 + half
         return pltpu.make_async_remote_copy(
             src_ref=src,
             dst_ref=dst,
@@ -213,14 +223,14 @@
         )
 
     def start_arrival(slot):
-        if slot == 0:
-            src, dst = times_ref.at[1 - half], swap_in
-        elif slot == 1:
-            src, dst = speed_ref, swap_speed
-        elif slot < 4:
-            src, dst = times_ref.at[0, pl.ds(0, HALO)], halo_in.at[0, slot - 2]
-        else:
-            src, dst = speed_ref.at[pl.ds(0, HALO)], halo_speed.at[slot - 4]
+        kind, other = slot // 2, slot % 2
+        src, dst = (
+            ((times_ref.at[0], swap_in), (speed_ref, swap_speed))[other],
+            (times_ref.at[0, pl.ds(0, near)], halo_first.at[other]),
+            (speed_ref.at[pl.ds(0, near)], near_speed.at[other]),
+            (speed_ref.at[pl.ds(0, depth - near)], rest_speed.at[other]),
+            (speed_ref.at[pl.ds(0, far)], far_speed.at[other]),
+        )[kind]
         return pltpu.make_async_remote_copy(
             src_ref=src,
             dst_ref=dst,
@@ -230,7 +240,7 @@
             device_id_type=mesh_id,
         )
 
-    for j in (0, 2, 3, 1, 4, 5):
+    for j in (0, 2, 3, 1, 4, 5, 6, 7, 8, 9):
         start_copy(j).start()
 
     at_lower = line == 0
@@ -244,22 +254,23 @@
     )
     loads[2].wait()
     for i in range(depth):
-        tab[0, HALO + half * depth + i, inside] = own_times[i]
-        spd[HALO + half * depth + i] = speed_ref[i]
+        tab[0, ghost + half * depth + i, inside] = own_times[i]
+        spd[ghost + half * depth + i] = speed_ref[i]
     for slot in range(2):
         start_arrival(slot).wait_recv()
     for i in range(depth):
-        tab[0, HALO + (1 - half) * depth + i, inside] = swap_in[i]
-        spd[HALO + (1 - half) * depth + i] = swap_speed[i]
-
-    def place_halo(exchange, side):
-        for i in range(HALO):
-            tab[side, i, inside] = jnp.where(at_lower, BIG, halo_in[exchange, 0, i])
-            tab[side, HALO + own + i, inside] = jnp.where(at_upper, BIG, halo_in[exchange, 1, i])
+        tab[0, ghost + (1 - half) * depth + i, inside] = swap_in[i]
+        spd[ghost + (1 - half) * depth + i] = swap_speed[i]
+
+    def place_halo(arrived_planes, width, side):
+        for i in range(width):
+            below, above = ghost - width + i, ghost + own + i
+            tab[side, below, inside] = jnp.where(at_lower, BIG, arrived_planes[0, i])
+            tab[side, above, inside] = jnp.where(at_upper, BIG, arrived_planes[1, i])
 
     lane = lax.broadcasted_iota(jnp.int32, (rows, lanes), 1)
 
-    def plane_value(side, plane, ghost):
+    def plane_value(side, plane, rim):
         centre = tab[side, plane, inside]
         along_x = jnp.minimum(tab[side, plane - 1, inside], tab[side, plane + 1, inside])
         along_y = jnp.minimum(
@@ -269,26 +280,26 @@
         after = jnp.where(lane == lanes - 1, BIG, pltpu.roll(centre, lanes - 1, 1))
         along_z = jnp.minimum(before, after)
         value = jnp.minimum(centre, godunov(along_x, along_y, along_z, spd[plane]))
-        if not ghost:
+        if not rim:
             return value
-        outside = (at_lower & (plane < HALO)) | (at_upper & (plane >= HALO + own))
+        outside = (at_lower & (plane < ghost)) | (at_upper & (plane >= ghost + own))
         return jnp.maximum(value, jnp.where(outside, BIG, -BIG))
 
-    def sweep(side, total, first, store):
+    def sweep(side, total, first, store, rim=False):
         def one(j, carry):
-            store(first + j, plane_value(side, first + j, False))
+            store(first + j, plane_value(side, first + j, rim))
             return carry
 
         unroll = next(u for u in (4, 5, 3, 2, 1) if total % u == 0)
         lax.fori_loop(0, total, one, 0, unroll=unroll)
 
-    def sweep_edges(side, done):
+    def sweep_edges(side, done, width):
         def one(j, carry):
-            for plane in (done + 1 + j, HALO + own - 1 - done + j):
+            for plane in (ghost - width + 1 + done + j, ghost + own - 1 - done + j):
                 tab[1 - side, plane, inside] = plane_value(side, plane, True)
             return carry
 
-        lax.fori_loop(0, HALO, one, 0, unroll=2)
+        lax.fori_loop(0, width, one, 0, unroll=2)
 
     def into(side):
         def store(plane, value):
@@ -297,62 +308,68 @@
         return store
 
     def into_stage(plane, value):
-        place = plane - HALO
+        place = plane - ghost
         for j in range(stas):
             stage[(place // depth) * stas + j, place % depth] = value[piece * j : piece * (j + 1)]
 
-    def into_edge(side, exchange, lower):
+    def into_edge(side):
         def store(plane, value):
             tab[side, plane, inside] = value
-            edge_out[exchange, 0 if lower else 1, plane - (HALO if lower else own)] = value
+            edge_out[plane - ghost] = value
 
         return store
 
-    def halo_copy(exchange, lower):
+    def halo_copy(lower):
         slot = 1 if lower else 0
         return pltpu.make_async_remote_copy(
-            src_ref=edge_out.at[exchange - 1, 0 if lower else 1],
-            dst_ref=halo_in.at[exchange, slot],
-            send_sem=halo_send.at[exchange - 1, slot],
-            recv_sem=halo_recv.at[exchange - 1, slot],
+            src_ref=edge_out.at[pl.ds(0 if lower else own - ghost, ghost)],
+            dst_ref=halo_next.at[slot],
+            send_sem=halo_send.at[slot],
+            recv_sem=halo_recv.at[slot],
             device_id=at(line - 1 if lower else line + 1, half),
             device_id_type=mesh_id,
         )
 
-    def last_round(side, exchange):
-        sweep(side, HALO, HALO, into_edge(1 - side, exchange - 1, True))
-        halo_copy(exchange, True).start()
-        sweep(side, HALO, own, into_edge(1 - side, exchange - 1, False))
-        halo_copy(exchange, False).start()
-        sweep(side, own - 2 * HALO, 2 * HALO, into(1 - side))
-
-    exchanges = ROUNDS // HALO
     side = 0
-    for exchange in range(exchanges):
-        final = exchange == exchanges - 1
+    for block, width in enumerate(BLOCKS):
         start = side
-        for r in range(HALO - 1):
-            sweep(side, own - 2 - 2 * r, HALO + 1 + r, into(1 - side))
-            side = 1 - side
-        if exchange == 0:
+        for r in range(width - 1):
+            if own - 2 - 2 * r > 0:
+                sweep(side, own - 2 - 2 * r, ghost + 1 + r, into(1 - side))
+                side = 1 - side
+        if block == 0:
             for slot in range(2, 6):
                 start_arrival(slot).wait_recv()
-            for i in range(HALO):
-                spd[i] = halo_speed[0, i]
-                spd[HALO + own + i] = halo_speed[1, i]
+            for i in range(near):
+                spd[ghost - near + i] = near_speed[0, i]
+                spd[ghost + own + i] = near_speed[1, i]
         else:
+            for slot in range(6, 10):
+                start_arrival(slot).wait_recv()
+            for i in range(depth - near):
+                spd[far + i] = rest_speed[0, i]
+                spd[ghost + own + near + i] = rest_speed[1, i]
+            for i in range(far):
+                spd[i] = far_speed[0, i]
+                spd[ghost + own + depth + i] = far_speed[1, i]
             for lower in (True, False):
-                halo_copy(exchange, lower).wait()
+                halo_copy(lower).wait()
         side = start
-        place_halo(exchange, side)
-        for r in range(HALO - 1):
-            sweep_edges(side, r)
+        place_halo(halo_first if block == 0 else halo_next, width, side)
+        for r in range(width - 1):
+            if own - 2 - 2 * r >= 0:
+                sweep_edges(side, r, width)
+            else:
+                total = own + 2 * (width - 1 - r)
+                sweep(side, total, ghost - width + 1 + r, into(1 - side), True)
             side = 1 - side
-        if final:
-            sweep(side, own, HALO, into_stage)
+        if block == 0:
+            sweep(side, own, ghost, into_edge(1 - side))
+            for lower in (True, False):
+                halo_copy(lower).start()
+            side = 1 - side
         else:
-            last_round(side, exchange + 1)
-            side = 1 - side
+            sweep(side, own, ghost, into_stage)
 
     def block_copy(j):
         other = (member + j) % members
@@ -388,7 +405,7 @@
 
     lax.fori_loop(1, members, start_block, 0)
     arrived[station] = stage[member]
-    for j in range(6):
+    for j in range(10):
         start_copy(j).wait_send()
     lax.fori_loop(1, members, end_block, 0)
     refined_ref[...] = arrived[...]
@@ -398,11 +415,11 @@
     per_device, depth, rows, lanes = coarse_times.shape
     stas = lax.axis_size("sta")
     stations = per_device * stas
-    assert per_device == NEAR and ROUNDS % HALO == 0 and HALO <= depth
+    near, ghost = BLOCKS
+    own = NEAR * depth
+    assert per_device == NEAR and sum(BLOCKS) == ROUNDS and near < depth < ghost <= own
     piece = rows // stas
-    own = NEAR * depth
-    count = own + 2 * HALO
-    exchanges = ROUNDS // HALO
+    count = own + 2 * ghost
     plane = (rows, lanes)
     vmem = pl.BlockSpec(memory_space=pltpu.VMEM)
     dma = pltpu.SemaphoreType.DMA
@@ -434,15 +451,18 @@
             pltpu.VMEM((count,) + plane, jnp.float32),
             pltpu.VMEM((depth,) + plane, jnp.float32),
             pltpu.VMEM((depth,) + plane, jnp.float32),
-            pltpu.VMEM((exchanges, 2, HALO) + plane, jnp.float32),
-            pltpu.VMEM((2, HALO) + plane, jnp.float32),
-            pltpu.VMEM((exchanges - 1, 2, HALO) + plane, jnp.float32),
+            pltpu.VMEM((2, near) + plane, jnp.float32),
+            pltpu.VMEM((2, ghost) + plane, jnp.float32),
+            pltpu.VMEM((2, near) + plane, jnp.float32),
+            pltpu.VMEM((2, depth - near) + plane, jnp.float32),
+            pltpu.VMEM((2, ghost - depth) + plane, jnp.float32),
+            pltpu.VMEM((own,) + plane, jnp.float32),
             pltpu.VMEM((NEAR * stas, depth, piece, lanes), jnp.float32),
             pltpu.VMEM((stations, depth, piece, lanes), jnp.float32),
-            dma((6,)),
-            dma((6,)),
-            dma((exchanges - 1, 2)),
-            dma((exchanges - 1, 2)),
+            dma((10,)),
+            dma((10,)),
+            dma((2,)),
+            dma((2,)),
             dma((NEAR * stas,)),
             dma((stations,)),
         ],

time: 71 us -> 71.1 us (level)
    pallas_call x1, Pallas kernels: 23.1 us -> 24.7 us  [event_density(): pl.pallas_call(locate_kernel, out_shape=(jax.ShapeDtypeStruct((rows,) + w...]
    pallas_call x1, Pallas kernels: 45.2 us -> 43.6 us  [refined_tables(): pl.pallas_call(travel_kernel, out_shape=(jax.ShapeDtypeStruct((stations,...]
where the time goes in v7:
time: 71.1 us; the launch traced here: 70.9 us
  Pallas kernels  70.3 us (99%)
    pallas_call x1, Pallas kernels, refined_tables(): pl.pallas_call(travel_kernel, out_shape=(jax.ShapeDtypeStruct((stations,...  43.6 us
    pallas_call x1, Pallas kernels, event_density(): pl.pallas_call(locate_kernel, out_shape=(jax.ShapeDtypeStruct((rows,) + w...  24.7 us
    pallas_call x1, Pallas kernels, event_density(): pl.pallas_call(density_kernel, out_shape=(jax.ShapeDtypeStruct((events *...  1.94 us

profile of v7, /device:TPU:1, one launch (start us, length us, event | category | flops | bytes accessed | tf_op | source)
XLA Modules:
  0.0 70.9 jit_solution(11447015584611823025)
XLA Ops:
  0.6 43.6 %travel.1 = (f32[16,5,4,128]{3,2,1,0:T(4,128)S(1)}, f32[256,128]{1,0:T(8,128)S(1)}, f32[16,256,128]{2,1,0:T(8,128)S(1)}, f32[16,256,128]{2,1,0:T(8,128)S(1)}, f3...) custom-call(f32[2,5,32,128]{3,2,1,0:T(8,128)} %times_ref.1, s32[5,32,128]{2,1,0:T(8,128)} %map_hbm.1, f32[64]{0:T(128)} %slowness_hbm.1, ...), custom_call_target="tpu_custom_call" | custom-call | tf_op jit(solution)/shard_map/travel/pallas_call | solution.py:429
  44.2 24.7 %locate.1 = (f32[20,256,128]{2,1,0:T(8,128)S(1)}, f32[256,128]{1,0:T(8,128)S(1)}, f32[4,128]{1,0:T(4,128)S(1)}) custom-call(f32[320,128]{1,0:T(8,128)S(1)} %bitcast.4, f32[256,128]{1,0:T(8,128)S(1)} %get-tuple-element.14.mask_rows, f32[16,256,128]{2,1,0:T(8,128)S(1)} %get-tuple-element.15.arrival_ref, f32[16,256,128]{2,1,0:T(8,128)S(1)} %get-tuple-element.16.seen_ref, ...), custom_call_target="tpu_custom_call" | custom-call | tf_op jit(solution)/shard_map/locate/pallas_call | solution.py:681
  69.0 1.9 %density.1 = (f32[5120,128]{1,0:T(8,128)}, f32[16,5,4,128]{3,2,1,0:T(4,128)}) custom-call(f32[20,256,128]{2,1,0:T(8,128)S(1)} %get-tuple-element.19.weight_ref, f32[256,128]{1,0:T(8,128)S(1)} %get-tuple-element.20.peak_ref, f32[4,128]{1,0:T(4,128)S(1)} %get-tuple-element.21.stats_ref, f32[16,5,4,128]{3,2,1,0:T(4,128)S(1)} %get-tuple-element.13.refined_ref), custom_call_target="tpu_custom_call" | custom-call | tf_op jit(solution)/shard_map/density/pallas_call | solution.py:704

commit v8 on v7

--- a/solution.py
+++ b/solution.py
@@ -120,8 +120,8 @@
     sta = lax.axis_index("sta")
     stas = lax.axis_size("sta")
     lines = lax.axis_size("space") // NEAR
-    line = space // NEAR
-    half = space % NEAR
+    line = lax.div(space, NEAR)
+    half = lax.rem(space, NEAR)
     depth, rows, lanes = map_ref.shape
     own = NEAR * depth
     near, ghost = BLOCKS
@@ -150,16 +150,16 @@
         load.start()
 
     def at(other_line, other_half):
-        return {"space": ((other_line + lines) % lines) * NEAR + other_half, "sta": sta}
+        return {"space": lax.rem(other_line + lines, lines) * NEAR + other_half, "sta": sta}
 
     def member_at(other):
-        return {"space": line * NEAR + other // stas, "sta": other % stas}
+        return {"space": line * NEAR + lax.div(other, stas), "sta": lax.rem(other, stas)}
 
     barrier = pltpu.get_barrier_semaphore()
 
     def greet(j, carry):
         pl.semaphore_signal(
-            barrier, inc=1, device_id=member_at((member + j) % members), device_id_type=mesh_id
+            barrier, inc=1, device_id=member_at(lax.rem(member + j, members)), device_id_type=mesh_id
         )
         return carry
 
@@ -310,7 +310,7 @@
     def into_stage(plane, value):
         place = plane - ghost
         for j in range(stas):
-            stage[(place // depth) * stas + j, place % depth] = value[piece * j : piece * (j + 1)]
+            stage[(lax.div(place, depth)) * stas + j, lax.rem(place, depth)] = value[piece * j : piece * (j + 1)]
 
     def into_edge(side):
         def store(plane, value):
@@ -372,7 +372,7 @@
             sweep(side, own, ghost, into_stage)
 
     def block_copy(j):
-        other = (member + j) % members
+        other = lax.rem(member + j, members)
         return pltpu.make_async_remote_copy(
             src_ref=stage.at[other],
             dst_ref=arrived.at[station],
@@ -383,8 +383,8 @@
         )
 
     def block_arrival(j):
-        other = (member + j) % members
-        source = NEAR * (other % stas) + other // stas
+        other = lax.rem(member + j, members)
+        source = NEAR * (lax.rem(other, stas)) + lax.div(other, stas)
         return pltpu.make_async_remote_copy(
             src_ref=stage.at[other],
             dst_ref=arrived.at[source],
@@ -403,7 +403,8 @@
         block_arrival(j).wait_recv()
         return carry
 
-    lax.fori_loop(1, members, start_block, 0)
+    lax.fori_loop(members // 4, members, start_block, 0)
+    lax.fori_loop(1, members // 4, start_block, 0)
     arrived[station] = stage[member]
     for j in range(10):
         start_copy(j).wait_send()
@@ -495,16 +496,16 @@
     sta = lax.axis_index("sta")
     stas = lax.axis_size("sta")
     lines = lax.axis_size("space") // NEAR
-    line = space // NEAR
-    member = (space % NEAR) * stas + sta
+    line = lax.div(space, NEAR)
+    member = (lax.rem(space, NEAR)) * stas + sta
     members = NEAR * stas
 
     def member_id(k):
-        other = (member + k) % members
-        return {"space": line * NEAR + other // stas, "sta": other % stas}
+        other = lax.rem(member + k, members)
+        return {"space": line * NEAR + lax.div(other, stas), "sta": lax.rem(other, stas)}
 
     def line_id(k):
-        return {"space": ((line + k) % lines) * NEAR + space % NEAR, "sta": sta}
+        return {"space": lax.rem(line + k, lines) * NEAR + lax.rem(space, NEAR), "sta": sta}
 
     barrier = pltpu.get_barrier_semaphore()
 

time: 71.1 us -> 70.6 us (level)
  no operation moved by 1% of the time
where the time goes in v8:
time: 70.6 us; the launch traced here: 70.5 us
  Pallas kernels  69.8 us (99%)
    pallas_call x1, Pallas kernels, refined_tables(): pl.pallas_call(travel_kernel, out_shape=(jax.ShapeDtypeStruct((stations,...  43.3 us
    pallas_call x1, Pallas kernels, event_density(): pl.pallas_call(locate_kernel, out_shape=(jax.ShapeDtypeStruct((rows,) + w...  24.6 us
    pallas_call x1, Pallas kernels, event_density(): pl.pallas_call(density_kernel, out_shape=(jax.ShapeDtypeStruct((events *...  1.94 us

profile of v8, /device:TPU:1, one launch (start us, length us, event | category | flops | bytes accessed | tf_op | source)
XLA Modules:
  0.0 70.5 jit_solution(6405418200995427224)
XLA Ops:
  0.6 43.3 %travel.1 = (f32[16,5,4,128]{3,2,1,0:T(4,128)S(1)}, f32[256,128]{1,0:T(8,128)S(1)}, f32[16,256,128]{2,1,0:T(8,128)S(1)}, f32[16,256,128]{2,1,0:T(8,128)S(1)}, f3...) custom-call(f32[2,5,32,128]{3,2,1,0:T(8,128)} %times_ref.1, s32[5,32,128]{2,1,0:T(8,128)} %map_hbm.1, f32[64]{0:T(128)} %slowness_hbm.1, ...), custom_call_target="tpu_custom_call" | custom-call | tf_op jit(solution)/shard_map/travel/pallas_call | solution.py:430
  44.0 24.6 %locate.1 = (f32[20,256,128]{2,1,0:T(8,128)S(1)}, f32[256,128]{1,0:T(8,128)S(1)}, f32[4,128]{1,0:T(4,128)S(1)}) custom-call(f32[320,128]{1,0:T(8,128)S(1)} %bitcast.4, f32[256,128]{1,0:T(8,128)S(1)} %get-tuple-element.14.mask_rows, f32[16,256,128]{2,1,0:T(8,128)S(1)} %get-tuple-element.15.arrival_ref, f32[16,256,128]{2,1,0:T(8,128)S(1)} %get-tuple-element.16.seen_ref, ...), custom_call_target="tpu_custom_call" | custom-call | tf_op jit(solution)/shard_map/locate/pallas_call | solution.py:682
  68.5 1.9 %density.1 = (f32[5120,128]{1,0:T(8,128)}, f32[16,5,4,128]{3,2,1,0:T(4,128)}) custom-call(f32[20,256,128]{2,1,0:T(8,128)S(1)} %get-tuple-element.19.weight_ref, f32[256,128]{1,0:T(8,128)S(1)} %get-tuple-element.20.peak_ref, f32[4,128]{1,0:T(4,128)S(1)} %get-tuple-element.21.stats_ref, f32[16,5,4,128]{3,2,1,0:T(4,128)S(1)} %get-tuple-element.13.refined_ref), custom_call_target="tpu_custom_call" | custom-call | tf_op jit(solution)/shard_map/density/pallas_call | solution.py:705
